TPU v7x, 128 devices: a whole 4x4x4 slice. The times are simulated.
128 devices in a mesh: tm: 32 (over z, y, core), clus: 4 (over x).
Axes of the slice: x: 4, y: 4, z: 4, core: 2. Of those that a mesh axis runs over, the one named last changes fastest.
Arguments:
- right_side: float32 [15, 131072], P(None, ('tm', 'clus')), may hold values from -8 to 8
- transition: float32 [15, 15, 131072], P(None, None, ('tm', 'clus')), may hold values from -1.5 to 1.5
- precond: float32 [15, 15, 131072], P(None, None, ('tm', 'clus')), as said below
- slot_of: int32 [131072], P(('tm', 'clus')), may hold values from 0 to 1023, as said below
- cluster_id: int32 [32, 4096], P('tm', 'clus'), may hold values from 0 to 63, never falling along the last dimension, each value on 1 to 128 neighbouring positions
- damping: float32 [32, 64], P('tm'), may hold values from 0.3 to 3
- pair_first: int32 [32, 8192], P('tm', 'clus'), may hold values from 0 to 4095
- pair_second: int32 [32, 8192], P('tm', 'clus'), may hold values from 0 to 4095
- pair_blocks: float32 [15, 15, 32, 8192], P(None, None, 'tm', 'clus'), may hold values from -1.5 to 1.5
Outputs:
- solution_field: float32 [15, 131072], P(None, ('tm', 'clus'))
- residual: float32 [15, 131072], P(None, ('tm', 'clus'))
Inputs may be any that keep to these rules, and one draw needn't show every extreme that they name: `slot_of`: the 1024 entries of each device's block are a permutation of 0 to 1023. `cluster_id`: never falling along each group's keyframes. `precond`: each keyframe's block is symmetric positive definite.
All inputs are finite; a program needn't handle non-finite values.
Results may differ from a plain program's by a relative error of at most 0.00015.
Values sent between devices are 32-bit elements; how exact they have to be, the bound alone decides.
A program may use at most 128 MiB of HBM per device.

v0:
```python
import jax
import jax.numpy as jnp
from jax import lax
from jax.sharding import PartitionSpec as P

ITERS = 2


def from_behind(shard, axis, by):
    count = lax.axis_size(axis)
    pairs = [(i, i + by) for i in range(count) if 0 <= i + by < count]
    return lax.ppermute(shard, axis, pairs)


def batched(blocks, field):
    count = blocks.shape[1]
    total = blocks[:, 0, :] * field[0][None, :]
    for inner in range(1, count):
        total = total + blocks[:, inner, :] * field[inner][None, :]
    return total


def batched_back(blocks, field):
    count = blocks.shape[0]
    total = blocks[0, :, :] * field[0][None, :]
    for inner in range(1, count):
        total = total + blocks[inner, :, :] * field[inner][None, :]
    return total


def take_columns(field, index):
    return jnp.take(field.T, index, axis=0).T


def add_columns(values, index, count):
    return jax.ops.segment_sum(values.T, index, num_segments=count).T


def precond_dot(residual, scaled):
    return lax.psum(jnp.sum(residual * scaled), ("tm", "clus"))


def on_device(
    right_side,
    transition,
    precond,
    slot_of,
    cluster_id,
    damping,
    pair_first,
    pair_second,
    pair_blocks,
):
    rows = right_side.shape[0]
    width = right_side.shape[1]
    n_time = lax.axis_size("tm")
    n_clus = lax.axis_size("clus")
    share = width // n_time
    flat = lax.axis_index("tm") * n_clus + lax.axis_index("clus")
    final_dev = flat == n_time * n_clus - 1
    columns = jnp.arange(width)
    inverse = jax.ops.segment_sum(columns, slot_of, num_segments=width)
    blocks = pair_blocks.reshape(pair_blocks.shape[0], pair_blocks.shape[1], -1)
    heads = pair_first.reshape(-1)
    tails = pair_second.reshape(-1)
    labels = jnp.arange(damping.shape[1])
    lam = jnp.sum(jnp.where(cluster_id == labels[:, None], damping.reshape(-1, 1), 0.0), axis=0)
    keep_last = jnp.where((columns == width - 1) & final_dev, 0.0, 1.0)
    solution_field = jnp.zeros_like(right_side)
    residual = right_side
    scaled = batched(precond, residual)
    direction = scaled
    rz_now = precond_dot(residual, scaled)
    for step in range(ITERS):
        moved = batched(transition, direction)
        next_col = from_behind(direction[:, :1], ("tm", "clus"), -1)
        inertial_errors = (
            jnp.concatenate([direction[:, 1:], next_col], axis=1) - moved
        ) * keep_last[None, :]
        inertial_back = batched_back(transition, inertial_errors)
        prior = from_behind(inertial_errors[:, width - 1 :], ("tm", "clus"), 1)
        outgoing = take_columns(direction, inverse).reshape(rows, n_time, share)
        own = lax.all_to_all(outgoing, "tm", split_axis=1, concat_axis=1, tiled=True).reshape(
            rows, width
        )
        grouped = lax.all_gather(own, "clus", axis=1, tiled=True)
        count = grouped.shape[1]
        near = take_columns(grouped, heads)
        far = take_columns(grouped, tails)
        errors = near - batched(blocks, far)
        back = batched_back(blocks, errors)
        terms = add_columns(errors, heads, count) - add_columns(back, tails, count)
        mine = lax.psum_scatter(terms, "clus", scatter_dimension=1, tiled=True) + lam[None, :] * own
        returned = lax.all_to_all(
            mine.reshape(rows, n_time, share), "tm", split_axis=1, concat_axis=1, tiled=True
        ).reshape(rows, width)
        image = (
            jnp.concatenate([prior, inertial_errors[:, :-1]], axis=1)
            - inertial_back
            + take_columns(returned, slot_of)
        )
        alpha = rz_now / lax.psum(jnp.sum(direction * image), ("tm", "clus"))
        solution_field = solution_field + alpha * direction
        residual = residual - alpha * image
        if step + 1 < ITERS:
            scaled = batched(precond, residual)
            rz_next = precond_dot(residual, scaled)
            direction = scaled + rz_next / rz_now * direction
            rz_now = rz_next
    return (solution_field, residual)


def solution(mesh):
    placed = (
        P(None, ("tm", "clus")),
        P(None, None, ("tm", "clus")),
        P(None, None, ("tm", "clus")),
        P(("tm", "clus")),
        P("tm", "clus"),
        P("tm", None),
        P("tm", "clus"),
        P("tm", "clus"),
        P(None, None, "tm", "clus"),
    )
    return jax.shard_map(
        on_device,
        mesh=mesh,
        in_specs=placed,
        out_specs=(P(None, ("tm", "clus")), P(None, ("tm", "clus"))),
        check_vma=False,
    )
```

profile of v0, /device:TPU:1, one launch (start us, length us, event | category | flops | bytes accessed | tf_op | source)
XLA Modules:
  0.0 621.4 jit_solution(1290287435150159494)
XLA Ops:
  7.2 4.8 fusion.90
  23.6 4.7 fusion.40
  28.8 5.8 collective-permute-start
  34.6 7.6 %scatter_custom_fusion = s32[1024]{0:T(1024)S(1)} fusion(s32[1024]{0:T(1024)S(1)} %copy-done.91, s32[1024]{0:T(1024)S(1)} %iota.12, s32[]{:T(128)} %constant.10.clone.1), kind=kCustom, calls=%fused_computation.343 | custom fusion | flops 1024 | bytes 4100 | tf_op jit(solution)/shard_map/scatter-add | solution.py:62
  42.2 2.8 gather_fusion
  46.3 8.2 %all-to-all-start = ((f32[32,1,480]{2,1,0:T(1,128)}), f32[32,1,480]{2,1,0:T(1,128)S(1)}, u32[]{:S(2)}, u32[]{:S(2)}) async-start(f32[32,1,480]{2,1,0:T(1,128)} %reshape.345), calls=%async_computation | async-start | bytes 131072 | tf_op jit(solution)/shard_map/all_to_all | solution.py:83
  54.9 4.6 slice_reduce_fusion.104
  60.1 9.1 %copy.274 = f32[15,15,1,2048]{0,3,1,2:T(8,128)} copy(f32[15,15,1,2048]{3,2,1,0:T(1,128)S(1)} %copy-done.4) | data formatting | bytes 3686400 | tf_op args[8]
  76.0 21.0 %all_gather.6 = f32[15,4096]{0,1:T(8,128)S(1)} all-gather(f32[15,1024]{0,1:T(8,128)S(1)} %bitcast.771), channel_id=1, replica_groups=mesh['tm'=32,'clus'=4] {'clus'}, dimensions={1}, use_global_device_ids=true | all-gather | bytes 307200 | tf_op jit(solution)/shard_map/all_gather | solution.py:86
  97.0 7.6 %gather_fusion.2 = f32[2048,15]{1,0:T(8,128)} fusion(f32[4096,15]{1,0:T(8,128)S(1)} %bitcast.762, s32[2048]{0:T(1024)S(1)} %fusion.79), kind=kCustom, calls=%fused_computation.5.clone | custom fusion | bytes 253952 | tf_op jit(solution)/shard_map/jit(_take)/gather | solution.py:32
  106.1 8.1 %slice_reduce_fusion.59 = (f32[2048]{0:T(1024)S(1)}, f32[2048]{0:T(1024)S(1)}, f32[2048]{0:T(1024)S(1)}, f32[2048]{0:T(1024)S(1)}, f32[2048]{0:T(1024)S(1)}, /*i...) fusion(f32[15,2048]{0,1:T(8,128)S(1)} %select_bitcast_fusion.1), kind=kLoop, calls=%fused_computation.88 | loop fusion | bytes 245760 | tf_op jit(solution)/shard_map/slice | solution.py:17
  114.2 7.6 %gather_fusion.1 = f32[2048,15]{1,0:T(8,128)} fusion(f32[4096,15]{1,0:T(8,128)S(1)} %bitcast.763, s32[2048]{0:T(1024)S(1)} %fusion.78), kind=kCustom, calls=%fused_computation.1.clone | custom fusion | bytes 253952 | tf_op jit(solution)/shard_map/jit(_take)/gather | solution.py:32
  121.8 10.2 %bitcast_subtract_fusion.1 = f32[15,2048]{0,1:T(8,128)S(1)} fusion(f32[2048,15]{1,0:T(8,128)} %gather_fusion.1, f32[15,15,2048]{0,2,1:T(8,128)} %bitcast.766, f32[2048]{0:T(1024)S(1)} %get-tuple-element.58, f32[2048]{0:T(1024)S(1)} %get-tuple-element.59, f32[2048]{0:T(1024)S(1)} %get-tuple-element.60, f32[2048]{0:T(1024)S(1)} %get-tuple-element.61, ...), kind=kLoop, calls=%fused_computation.95 | loop fusion | flops 952320 | bytes 2213888 | tf_op jit(solution)/shard_map/sub | solution.py:90
  132.1 8.1 %slice_reduce_fusion.44 = (f32[2048]{0:T(1024)S(1)}, f32[2048]{0:T(1024)S(1)}, f32[2048]{0:T(1024)S(1)}, f32[2048]{0:T(1024)S(1)}, f32[2048]{0:T(1024)S(1)}, /*i...) fusion(f32[15,2048]{0,1:T(8,128)S(1)} %bitcast_subtract_fusion.1), kind=kLoop, calls=%fused_computation.59 | loop fusion | bytes 245760 | tf_op jit(solution)/shard_map/slice | solution.py:25
  141.9 2.2 copy.289
  144.1 13.5 %scatter_custom_fusion.1 = f32[4096,15]{1,0:T(8,128)} fusion(s32[2048]{0:T(1024)S(1)} %bitcast.789, f32[15,2048]{0,1:T(8,128)S(1)} %bitcast_subtract_fusion.1, f32[]{:T(128)} %constant.25.clone.1), kind=kCustom, calls=%fused_computation.93 | custom fusion | flops 30720 | bytes 1294340 | tf_op jit(solution)/shard_map/scatter-add | solution.py:36
  157.6 13.4 %scatter_custom_fusion.2 = f32[4096,15]{1,0:T(8,128)} fusion(s32[2048]{0:T(1024)} %bitcast.790, f32[2048,15]{1,0:T(8,128)} %copy.289, f32[]{:T(128)} %constant.25.clone.1), kind=kCustom, calls=%fused_computation.101 | custom fusion | flops 30720 | bytes 246272 | tf_op jit(solution)/shard_map/scatter-add | solution.py:36
  171.0 3.1 subtract_bitcast_fusion.1
  199.0 5.0 reduce-scatter.3.cloned.1.call-done
  208.3 7.8 %all-to-all-start.1 = ((f32[32,1,480]{2,1,0:T(1,128)}), f32[32,1,480]{2,1,0:T(1,128)S(1)}, u32[]{:S(2)}, u32[]{:S(2)}) async-start(f32[32,1,480]{2,1,0:T(1,128)} %reshape.347), calls=%async_computation.2 | async-start | bytes 131072 | tf_op jit(solution)/shard_map/all_to_all | solution.py:94
  218.2 5.3 all-to-all-done.1
  226.2 4.0 gather_fusion.3
  230.3 7.0 %multiply_reduce_fusion.2 = (f32[]{:T(128)}, f32[]{:T(128)}, f32[15,1024]{0,1:T(8,128)}) fusion(f32[15,1024]{0,1:T(8,128)S(1)} %fusion.40, f32[15,1024]{0,1:T(8,128)} %copy.238, f32[1024,15]{1,0:T(8,128)} %gather_fusion.3, pred[1024]{0:T(1024)(128)(4,1)} %compare_and_fusion.2, f32[15,1024]{0,1:T(8,128)} %copy.271, f32[1024]{0:T(1024)S(1)} %bitcast.810, ...), kind=kLoop, calls=%fused_computation.276 | loop fusion | flops 552958 | bytes 1291272 | tf_op jit(solution)/shard_map/reduce_sum | solution.py:102
  237.2 62.9 %all-reduce = (f32[]{:T(128)}, f32[]{:T(128)}) all-reduce(f32[]{:T(128)} %get-tuple-element.103, f32[]{:T(128)} %get-tuple-element.102), channel_id=1, replica_groups=mesh['tm'=32,'clus'=4] {'tm','clus'}, use_global_device_ids=true, to_apply=%region_1.2 | all-reduce | flops 2 | bytes 16 | tf_op jit(solution)/shard_map/psum | solution.py:40
  302.8 4.0 slice_reduce_fusion.89
  306.9 3.2 multiply_reduce_fusion.1
  310.1 63.0 %psum.30 = f32[]{:T(128)} all-reduce(f32[]{:T(128)} %get-tuple-element.123), channel_id=1, replica_groups=mesh['tm'=32,'clus'=4] {'tm','clus'}, use_global_device_ids=true, to_apply=%region_10.13 | all-reduce | flops 1 | bytes 8 | tf_op jit(solution)/shard_map/psum | solution.py:40
  374.5 2.8 gather_fusion.4
  378.0 12.0 %all_to_all.20 = f32[32,1,480]{2,1,0:T(1,128)S(1)} all-to-all(f32[32,1,480]{2,1,0:T(1,128)S(1)} %reshape.349), channel_id=1, replica_groups=mesh['tm'=32,'clus'=4] {'tm'}, dimensions={0} | all-to-all | bytes 122880 | tf_op jit(solution)/shard_map/all_to_all | solution.py:83
  392.0 20.8 %all_gather.7 = f32[15,4096]{0,1:T(8,128)S(1)} all-gather(f32[15,1024]{0,1:T(8,128)} %bitcast.770), channel_id=1, replica_groups=mesh['tm'=32,'clus'=4] {'clus'}, dimensions={1}, use_global_device_ids=true | all-gather | bytes 307200 | tf_op jit(solution)/shard_map/all_gather | solution.py:86
  412.8 7.8 %gather_fusion.6 = f32[2048,15]{1,0:T(8,128)} fusion(f32[4096,15]{1,0:T(8,128)S(1)} %bitcast.764, s32[2048]{0:T(1024)S(1)} %fusion.79), kind=kCustom, calls=%fused_computation.7.clone | custom fusion | bytes 253952 | tf_op jit(solution)/shard_map/jit(_take)/gather | solution.py:32
  420.6 7.6 %gather_fusion.5 = f32[2048,15]{1,0:T(8,128)} fusion(f32[4096,15]{1,0:T(8,128)S(1)} %bitcast.765, s32[2048]{0:T(1024)S(1)} %fusion.78), kind=kCustom, calls=%fused_computation.6.clone | custom fusion | bytes 253952 | tf_op jit(solution)/shard_map/jit(_take)/gather | solution.py:32
  429.8 8.1 %slice_reduce_fusion.29 = (f32[2048]{0:T(1024)S(1)}, f32[2048]{0:T(1024)S(1)}, f32[2048]{0:T(1024)S(1)}, f32[2048]{0:T(1024)S(1)}, f32[2048]{0:T(1024)S(1)}, /*i...) fusion(f32[15,2048]{0,1:T(8,128)S(1)} %select_bitcast_fusion), kind=kLoop, calls=%fused_computation.44 | loop fusion | bytes 245760 | tf_op jit(solution)/shard_map/slice | solution.py:17
  437.9 10.1 %bitcast_subtract_fusion = f32[15,2048]{0,1:T(8,128)S(1)} fusion(f32[2048,15]{1,0:T(8,128)S(1)} %copy-done.36, f32[15,15,2048]{0,2,1:T(8,128)} %bitcast.767, f32[2048]{0:T(1024)S(1)} %get-tuple-element.28, f32[2048]{0:T(1024)S(1)} %get-tuple-element.29, f32[2048]{0:T(1024)S(1)} %get-tuple-element.30, f32[2048]{0:T(1024)S(1)} %get-tuple-element.31, ...), kind=kLoop, calls=%fused_computation.92 | loop fusion | flops 952320 | bytes 2213888 | tf_op jit(solution)/shard_map/sub | solution.py:90
  448.0 8.7 %slice_reduce_fusion.14 = (f32[2048]{0:T(1024)S(1)}, f32[2048]{0:T(1024)S(1)}, f32[2048]{0:T(1024)S(1)}, f32[2048]{0:T(1024)S(1)}, f32[2048]{0:T(1024)S(1)}, /*i...) fusion(f32[15,2048]{0,1:T(8,128)S(1)} %bitcast_subtract_fusion), kind=kLoop, calls=%fused_computation.29 | loop fusion | bytes 245760 | tf_op jit(solution)/shard_map/slice | solution.py:25
  456.7 13.4 %scatter_custom_fusion.3 = f32[4096,15]{1,0:T(8,128)} fusion(s32[2048]{0:T(1024)} %bitcast.786, f32[15,2048]{0,1:T(8,128)S(1)} %bitcast_subtract_fusion, f32[]{:T(128)} %constant.25.clone.1), kind=kCustom, calls=%fused_computation.90 | custom fusion | flops 30720 | bytes 369152 | tf_op jit(solution)/shard_map/scatter-add | solution.py:36
  470.2 2.7 fusion.75
  472.9 2.4 copy.298
  475.3 13.2 %scatter_custom_fusion.4 = f32[4096,15]{1,0:T(8,128)} fusion(s32[2048]{0:T(1024)} %bitcast.791, f32[2048,15]{1,0:T(8,128)} %copy.298, f32[]{:T(128)} %constant.25.clone.1), kind=kCustom, calls=%fused_computation.98 | custom fusion | flops 30720 | bytes 246272 | tf_op jit(solution)/shard_map/scatter-add | solution.py:36
  488.5 3.1 subtract_bitcast_fusion
  491.8 4.0 slice_reduce_fusion.74
  495.9 4.0 collective-permute-start.2
  503.3 14.8 %reduce-scatter.5.cloned.1.call-done = f32[15,1024]{0,1:T(8,128)} async-done(((f32[15,4096]{0,1:T(8,128)}), f32[15,1024]{0,1:T(8,128)}) %reduce-scatter.5.cloned.1.call-update) | async-done | bytes 61456 | tf_op jit(solution)/shard_map/reduce_scatter | solution.py:93
  520.4 7.8 %all-to-all-start.3 = ((f32[32,1,480]{2,1,0:T(1,128)}), f32[32,1,480]{2,1,0:T(1,128)S(1)}, u32[]{:S(2)}, u32[]{:S(2)}) async-start(f32[32,1,480]{2,1,0:T(1,128)} %reshape.351), calls=%async_computation.5 | async-start | bytes 131072 | tf_op jit(solution)/shard_map/all_to_all | solution.py:94
  529.4 6.1 all-to-all-done.3
  536.7 4.0 gather_fusion.7
  540.8 6.5 %multiply_reduce_fusion = (f32[]{:T(128)}, f32[15,1024]{0,1:T(8,128)}) fusion(f32[15,1024]{0,1:T(8,128)S(1)} %multiply_add_fusion.2, f32[1024,15]{1,0:T(8,128)} %gather_fusion.7, pred[1024]{0:T(1024)(128)(4,1)S(1)} %copy-done.92, f32[15,1024]{0,1:T(8,128)} %copy.295, f32[1024]{0:T(1024)S(1)} %bitcast.795, f32[1,15,1024]{1,2,0:T(8,128)} %copy.349, ...), kind=kLoop, calls=%fused_computation.271 | loop fusion | flops 522239 | bytes 1229828 | tf_op jit(solution)/shard_map/reduce_sum | solution.py:102
  547.3 62.7 %psum.31 = f32[]{:T(128)} all-reduce(f32[]{:T(128)} %get-tuple-element.121), channel_id=1, replica_groups=mesh['tm'=32,'clus'=4] {'tm','clus'}, use_global_device_ids=true, to_apply=%region_15.18 | all-reduce | flops 1 | bytes 8 | tf_op jit(solution)/shard_map/psum | solution.py:102
  (302 shorter events, 74.1 us)
Async XLA Ops:
  12.2 11.3 %copy-start.12 = (f32[15,1,1024]{0,2,1:T(8,128)}, f32[15,1,1024]{0,2,1:T(8,128)S(1)}, u32[]{:S(2)}) copy-start(f32[15,1,1024]{0,2,1:T(8,128)S(1)} %copy.304) | copy-start | bytes 184324
  12.4 11.1 %copy-start.14 = (f32[15,1,1024]{0,2,1:T(8,128)}, f32[15,1,1024]{0,2,1:T(8,128)S(1)}, u32[]{:S(2)}) copy-start(f32[15,1,1024]{0,2,1:T(8,128)S(1)} %copy.305) | copy-start | bytes 184324
  12.7 10.9 %copy-start.16 = (f32[15,1,1024]{0,2,1:T(8,128)}, f32[15,1,1024]{0,2,1:T(8,128)S(1)}, u32[]{:S(2)}) copy-start(f32[15,1,1024]{0,2,1:T(8,128)S(1)} %copy.306) | copy-start | bytes 184324
  12.9 10.6 %copy-start.18 = (f32[15,1,1024]{0,2,1:T(8,128)}, f32[15,1,1024]{0,2,1:T(8,128)S(1)}, u32[]{:S(2)}) copy-start(f32[15,1,1024]{0,2,1:T(8,128)S(1)} %copy.307) | copy-start | bytes 184324
  13.2 10.4 %copy-start.20 = (f32[15,1,1024]{0,2,1:T(8,128)}, f32[15,1,1024]{0,2,1:T(8,128)S(1)}, u32[]{:S(2)}) copy-start(f32[15,1,1024]{0,2,1:T(8,128)S(1)} %copy.308) | copy-start | bytes 184324
  23.6 11.0 %copy-start.91 = (s32[1024]{0:T(1024)S(1)}, s32[1024]{0:T(1024)}, u32[]{:S(2)}) copy-start(s32[1024]{0:T(1024)} %param.16) | copy-start | bytes 12292
  28.8 164.7 %collective-permute-start = (f32[15,1]{0,1:T(1,128)}, f32[15,1]{0,1:T(1,128)}, u32[]{:S(2)}, u32[]{:S(2)}) collective-permute-start(f32[15,1]{0,1:T(1,128)} %slice.1039), channel_id=1, source_target_pairs={{1,0},{2,1},{3,2},{4,3},{5,4},{6,5},{7,6},{8,7},{9,8},{10,9},{11,1... | collective-permute-start | bytes 188 | tf_op jit(solution)/shard_map/ppermute | solution.py:12
  46.3 27.9 %all-to-all-start = ((f32[32,1,480]{2,1,0:T(1,128)}), f32[32,1,480]{2,1,0:T(1,128)S(1)}, u32[]{:S(2)}, u32[]{:S(2)}) async-start(f32[32,1,480]{2,1,0:T(1,128)} %reshape.345), calls=%async_computation | async-start | bytes 131072 | tf_op jit(solution)/shard_map/all_to_all | solution.py:83
  54.6 149.5 %reduce-scatter.3.cloned.1.call-start = ((), (), s32[]{:S(2)}) async-start(), calls=%async_computation.6 | async-start | bytes 2621440 | tf_op jit(solution)/shard_map/reduce_scatter | solution.py:93
  60.1 61.7 %copy-start.88 = (pred[2048]{0:T(1024)(128)(4,1)}, pred[2048]{0:T(1024)(128)(4,1)S(1)}, u32[]{:S(2)}) copy-start(pred[2048]{0:T(1024)(128)(4,1)S(1)} %compare_and_fusion.1) | copy-start | bytes 6148
  76.0 28.6 %copy-start.33 = (f32[15,32,32]{0,2,1:T(8,128)}, f32[15,32,32]{0,2,1:T(8,128)S(1)}, u32[]{:S(2)}) copy-start(f32[15,32,32]{0,2,1:T(8,128)S(1)} %copy.273) | copy-start | bytes 184324
  157.6 13.4 %copy-start.3 = (f32[4096,15]{1,0:T(8,128)S(1)}, f32[4096,15]{1,0:T(8,128)}, u32[]{:S(2)}) copy-start(f32[4096,15]{1,0:T(8,128)} %scatter_custom_fusion.1) | copy-start | bytes 737284
  177.1 53.1 %copy-start.5 = (f32[1,15,1024]{1,2,0:T(8,128)}, f32[1,15,1024]{1,2,0:T(8,128)S(1)}, u32[]{:S(2)}) copy-start(f32[1,15,1024]{1,2,0:T(8,128)S(1)} %copy.335) | copy-start | bytes 184324
  177.3 52.9 %copy-start.7 = (f32[1,15,1024]{1,2,0:T(8,128)}, f32[1,15,1024]{1,2,0:T(8,128)S(1)}, u32[]{:S(2)}) copy-start(f32[1,15,1024]{1,2,0:T(8,128)S(1)} %copy.336) | copy-start | bytes 184324
  177.6 52.6 %copy-start.9 = (f32[1,15,1024]{1,2,0:T(8,128)}, f32[1,15,1024]{1,2,0:T(8,128)S(1)}, u32[]{:S(2)}) copy-start(f32[1,15,1024]{1,2,0:T(8,128)S(1)} %copy.337) | copy-start | bytes 184324
  177.8 52.4 %copy-start.11 = (f32[1,15,1024]{1,2,0:T(8,128)}, f32[1,15,1024]{1,2,0:T(8,128)S(1)}, u32[]{:S(2)}) copy-start(f32[1,15,1024]{1,2,0:T(8,128)S(1)} %copy.338) | copy-start | bytes 184324
  184.1 19.9 %copy-start.34 = (f32[15,32,32]{0,2,1:T(8,128)S(1)}, f32[15,32,32]{0,2,1:T(8,128)}, u32[]{:S(2)}) copy-start(f32[15,32,32]{0,2,1:T(8,128)} %copy-done.33) | copy-start | bytes 184324
  196.5 19.7 %collective-permute-start.1 = (f32[15,1]{1,0:T(8,128)}, f32[15,1]{1,0:T(8,128)}, u32[]{:S(2)}, u32[]{:S(2)}) collective-permute-start(f32[15,1]{1,0:T(8,128)} %slice.1055), channel_id=1, source_target_pairs={{0,1},{1,2},{2,3},{3,4},{4,5},{5,6},{6,7},{7,8},{8,9},{9,10},{10,1... | collective-permute-start | bytes 188 | tf_op jit(solution)/shard_map/ppermute | solution.py:12
  208.3 15.2 %all-to-all-start.1 = ((f32[32,1,480]{2,1,0:T(1,128)}), f32[32,1,480]{2,1,0:T(1,128)S(1)}, u32[]{:S(2)}, u32[]{:S(2)}) async-start(f32[32,1,480]{2,1,0:T(1,128)} %reshape.347), calls=%async_computation.2 | async-start | bytes 131072 | tf_op jit(solution)/shard_map/all_to_all | solution.py:94
  216.1 302.0 %reduce-scatter.5.cloned.1.call-start = ((), (), s32[]{:S(2)}) async-start(), calls=%async_computation.7 | async-start | bytes 2621440 | tf_op jit(solution)/shard_map/reduce_scatter | solution.py:93
  230.2 71.2 %copy-start.35 = (f32[15,1024]{0,1:T(8,128)S(1)}, f32[15,1024]{0,1:T(8,128)}, u32[]{:S(2)}) copy-start(f32[15,1024]{0,1:T(8,128)} %copy.238) | copy-start | bytes 184324
  456.6 13.5 %copy-start.39 = (f32[1,15,1,2048]{3,2,1,0:T(1,128)S(1)}, f32[1,15,1,2048]{3,2,1,0:T(1,128)}, u32[]{:S(2)}) copy-start(f32[1,15,1,2048]{3,2,1,0:T(1,128)} %get-tuple-element.129) | copy-start | bytes 368644
  456.6 13.5 %copy-start.41 = (f32[1,15,1,2048]{3,2,1,0:T(1,128)S(1)}, f32[1,15,1,2048]{3,2,1,0:T(1,128)}, u32[]{:S(2)}) copy-start(f32[1,15,1,2048]{3,2,1,0:T(1,128)} %get-tuple-element.130) | copy-start | bytes 368644
  456.6 13.5 %copy-start.43 = (f32[1,15,1,2048]{3,2,1,0:T(1,128)S(1)}, f32[1,15,1,2048]{3,2,1,0:T(1,128)}, u32[]{:S(2)}) copy-start(f32[1,15,1,2048]{3,2,1,0:T(1,128)} %get-tuple-element.131) | copy-start | bytes 368644
  456.6 13.5 %copy-start.45 = (f32[1,15,1,2048]{3,2,1,0:T(1,128)S(1)}, f32[1,15,1,2048]{3,2,1,0:T(1,128)}, u32[]{:S(2)}) copy-start(f32[1,15,1,2048]{3,2,1,0:T(1,128)} %get-tuple-element.132) | copy-start | bytes 368644
  456.6 13.5 %copy-start.47 = (f32[1,15,1,2048]{3,2,1,0:T(1,128)S(1)}, f32[1,15,1,2048]{3,2,1,0:T(1,128)}, u32[]{:S(2)}) copy-start(f32[1,15,1,2048]{3,2,1,0:T(1,128)} %get-tuple-element.133) | copy-start | bytes 368644
  456.6 13.5 %copy-start.49 = (f32[1,15,1,2048]{3,2,1,0:T(1,128)S(1)}, f32[1,15,1,2048]{3,2,1,0:T(1,128)}, u32[]{:S(2)}) copy-start(f32[1,15,1,2048]{3,2,1,0:T(1,128)} %get-tuple-element.134) | copy-start | bytes 368644
  456.6 13.5 %copy-start.51 = (f32[1,15,1,2048]{3,2,1,0:T(1,128)S(1)}, f32[1,15,1,2048]{3,2,1,0:T(1,128)}, u32[]{:S(2)}) copy-start(f32[1,15,1,2048]{3,2,1,0:T(1,128)} %get-tuple-element.135) | copy-start | bytes 368644
  456.6 13.5 %copy-start.53 = (f32[1,15,1,2048]{3,2,1,0:T(1,128)S(1)}, f32[1,15,1,2048]{3,2,1,0:T(1,128)}, u32[]{:S(2)}) copy-start(f32[1,15,1,2048]{3,2,1,0:T(1,128)} %get-tuple-element.136) | copy-start | bytes 368644
  472.9 15.6 %copy-start.2 = (f32[4096,15]{1,0:T(8,128)S(1)}, f32[4096,15]{1,0:T(8,128)}, u32[]{:S(2)}) copy-start(f32[4096,15]{1,0:T(8,128)} %scatter_custom_fusion.3) | copy-start | bytes 737284
  491.6 9.2 %copy-start.59 = (f32[15,1,1024]{2,1,0:T(1,128)S(1)}, f32[15,1,1024]{2,1,0:T(1,128)}, u32[]{:S(2)}) copy-start(f32[15,1,1024]{2,1,0:T(1,128)} %get-tuple-element.156) | copy-start | bytes 184324
  491.6 9.2 %copy-start.60 = (f32[15,1,1024]{2,1,0:T(1,128)S(1)}, f32[15,1,1024]{2,1,0:T(1,128)}, u32[]{:S(2)}) copy-start(f32[15,1,1024]{2,1,0:T(1,128)} %get-tuple-element.157) | copy-start | bytes 184324
  491.6 9.2 %copy-start.61 = (f32[15,1,1024]{2,1,0:T(1,128)S(1)}, f32[15,1,1024]{2,1,0:T(1,128)}, u32[]{:S(2)}) copy-start(f32[15,1,1024]{2,1,0:T(1,128)} %get-tuple-element.158) | copy-start | bytes 184324
  491.7 9.2 %copy-start.62 = (f32[15,1,1024]{2,1,0:T(1,128)S(1)}, f32[15,1,1024]{2,1,0:T(1,128)}, u32[]{:S(2)}) copy-start(f32[15,1,1024]{2,1,0:T(1,128)} %get-tuple-element.159) | copy-start | bytes 184324
  491.7 9.2 %copy-start.63 = (f32[15,1,1024]{2,1,0:T(1,128)S(1)}, f32[15,1,1024]{2,1,0:T(1,128)}, u32[]{:S(2)}) copy-start(f32[15,1,1024]{2,1,0:T(1,128)} %get-tuple-element.160) | copy-start | bytes 184324
  491.7 9.2 %copy-start.64 = (f32[15,1,1024]{2,1,0:T(1,128)S(1)}, f32[15,1,1024]{2,1,0:T(1,128)}, u32[]{:S(2)}) copy-start(f32[15,1,1024]{2,1,0:T(1,128)} %get-tuple-element.161) | copy-start | bytes 184324
  491.7 9.2 %copy-start.65 = (f32[15,1,1024]{2,1,0:T(1,128)S(1)}, f32[15,1,1024]{2,1,0:T(1,128)}, u32[]{:S(2)}) copy-start(f32[15,1,1024]{2,1,0:T(1,128)} %get-tuple-element.162) | copy-start | bytes 184324
  491.7 9.2 %copy-start.66 = (f32[15,1,1024]{2,1,0:T(1,128)S(1)}, f32[15,1,1024]{2,1,0:T(1,128)}, u32[]{:S(2)}) copy-start(f32[15,1,1024]{2,1,0:T(1,128)} %get-tuple-element.163) | copy-start | bytes 184324
  491.7 9.2 %copy-start.67 = (f32[15,1,1024]{2,1,0:T(1,128)S(1)}, f32[15,1,1024]{2,1,0:T(1,128)}, u32[]{:S(2)}) copy-start(f32[15,1,1024]{2,1,0:T(1,128)} %get-tuple-element.164) | copy-start | bytes 184324
  491.7 9.2 %copy-start.68 = (f32[15,1,1024]{2,1,0:T(1,128)S(1)}, f32[15,1,1024]{2,1,0:T(1,128)}, u32[]{:S(2)}) copy-start(f32[15,1,1024]{2,1,0:T(1,128)} %get-tuple-element.165) | copy-start | bytes 184324
  491.7 9.2 %copy-start.69 = (f32[15,1,1024]{2,1,0:T(1,128)S(1)}, f32[15,1,1024]{2,1,0:T(1,128)}, u32[]{:S(2)}) copy-start(f32[15,1,1024]{2,1,0:T(1,128)} %get-tuple-element.166) | copy-start | bytes 184324
  491.7 9.2 %copy-start.70 = (f32[15,1,1024]{2,1,0:T(1,128)S(1)}, f32[15,1,1024]{2,1,0:T(1,128)}, u32[]{:S(2)}) copy-start(f32[15,1,1024]{2,1,0:T(1,128)} %get-tuple-element.167) | copy-start | bytes 184324
  491.7 9.2 %copy-start.71 = (f32[15,1,1024]{2,1,0:T(1,128)S(1)}, f32[15,1,1024]{2,1,0:T(1,128)}, u32[]{:S(2)}) copy-start(f32[15,1,1024]{2,1,0:T(1,128)} %get-tuple-element.168) | copy-start | bytes 184324
  495.8 22.3 %copy-start.32 = (f32[15,32,32]{0,2,1:T(8,128)S(1)}, f32[15,32,32]{0,2,1:T(8,128)}, u32[]{:S(2)}) copy-start(f32[15,32,32]{0,2,1:T(8,128)} %copy.297) | copy-start | bytes 184324
  495.9 4.9 collective-permute-start.2
  501.3 26.9 %collective-permute-start.3 = (f32[15,1]{1,0:T(8,128)S(1)}, f32[15,1]{1,0:T(8,128)S(1)}, u32[]{:S(2)}, u32[]{:S(2)}) collective-permute-start(f32[15,1]{1,0:T(8,128)S(1)} %slice.1149), channel_id=1, source_target_pairs={{0,1},{1,2},{2,3},{3,4},{4,5},{5,6},{6,7},{7,8},{8,9},{9,10},{10,1... | collective-permute-start | bytes 188 | tf_op jit(solution)/shard_map/ppermute | solution.py:12
  520.4 15.1 %all-to-all-start.3 = ((f32[32,1,480]{2,1,0:T(1,128)}), f32[32,1,480]{2,1,0:T(1,128)S(1)}, u32[]{:S(2)}, u32[]{:S(2)}) async-start(f32[32,1,480]{2,1,0:T(1,128)} %reshape.351), calls=%async_computation.5 | async-start | bytes 131072 | tf_op jit(solution)/shard_map/all_to_all | solution.py:94
  540.8 70.6 %copy-start.1 = (f32[15,1024]{0,1:T(8,128)S(1)}, f32[15,1024]{0,1:T(8,128)}, u32[]{:S(2)}) copy-start(f32[15,1024]{0,1:T(8,128)} %copy-done) | copy-start | bytes 184324
  (58 other events, 302.2 us)
Sparse Core Ops, SparseCore 0:
  174.3 29.7 reduce-scatter.2
  491.7 26.3 reduce-scatter.4
where the time goes:
time: 628 us; the launch traced here: 621 us
  blocking collectives  242 us (39%)
  local copies, waits for them, and re-layouts  160 us (25%)
  other arithmetic  130 us (21%)
  starting transfers between devices  37.7 us (6%)
  waiting for transfers between devices  32 us (5%)
  between operations  20.2 us (3%)
    psum x2, blocking collectives, precond_dot(): return lax.psum(jnp.sum(residual * scaled), ('tm', 'clus'))  126 us
    psum x1, blocking collectives, on_device(): alpha = rz_now / lax.psum(jnp.sum(direction * image), ('tm', 'clus'))  62.7 us
    scatter-add x4, other arithmetic, add_columns(): return jax.ops.segment_sum(values.T, index, num_segments=count).T  53.5 us
    unnamed x238, local copies, waits for them, and re-layouts  45.6 us
    gather x8, local copies, waits for them, and re-layouts, take_columns(): return jnp.take(field.T, index, axis=0).T  44.2 us
    all_gather x2, blocking collectives, on_device(): grouped = lax.all_gather(own, 'clus', axis=1, tiled=True)  41.7 us
    slice x7, local copies, waits for them, and re-layouts, batched(): total = blocks[:, 0, :] * field[0][None, :]  33.6 us
    sub x2, other arithmetic, on_device(): errors = near - batched(blocks, far)  20.3 us
  transfers between devices with their start and end apart: 9, of which 5 were waited for; matrix products, arithmetic and copies ran while one was open for 23% of the time, Pallas kernels for 0%

commit v1 on v0

v1 whole, which is shorter than its diff:
```python
import jax
import jax.numpy as jnp
from jax import lax
from jax.experimental import pallas as pl
from jax.experimental.pallas import tpu as pltpu
from jax.sharding import PartitionSpec as P

MESHID = pl.DeviceIdType.MESH
F32 = jnp.float32
BF16 = jnp.bfloat16
N = 15


def hops(d):
    return min(d, 4 - d)


RINGS = sorted(((z, y) for z in range(4) for y in range(4)), key=lambda a: -hops(a[0]) - hops(a[1]))


def sweep(action):
    tm = lax.axis_index("tm")
    cl = lax.axis_index("clus")
    z, y, core = tm // 8, (tm // 2) % 4, tm % 2
    for dz, dy in RINGS:
        row = ((z + dz) % 4) * 8 + ((y + dy) % 4) * 2
        first = 1 if (dz, dy) == (0, 0) else 0

        def one(i, c):
            action(row + (core + i // 4) % 2, (cl + i % 4) % 4)
            return c

        lax.fori_loop(first, 8, one, 0)


def iota(shape, axis):
    return lax.broadcasted_iota(jnp.int32, shape, axis)


def total(v):
    while v.ndim > 2:
        v = jnp.sum(v, axis=0)
    return jnp.sum(v, axis=(0, 1), keepdims=True)


def loop(n, body):
    def step(i, c):
        body(i)
        return c

    lax.fori_loop(0, n, step, 0)


def rows8(i):
    return pl.ds(pl.multiple_of(i * 8, 8), 8)


def rows16(i):
    return pl.ds(pl.multiple_of(i * 16, 16), 16)


def rows4(i):
    return pl.ds(pl.multiple_of(i * 4, 4), 4)


def lanes(i):
    return pl.ds(pl.multiple_of(i * 128, 128), 128)


def multiply(blocks, src, dst):
    field = src[0:120, :].reshape(N, 8, 128)

    def one(i):
        dst[rows8(i), :] = jnp.sum(blocks[i] * field, axis=0)

    loop(N, one)


def after(v):
    turned = pltpu.roll(v, 127, axis=1)
    return jnp.where(iota((8, 128), 1) == 127, pltpu.roll(turned, 7, axis=0), turned)


def before(v):
    turned = pltpu.roll(v, 1, axis=1)
    return jnp.where(iota((8, 128), 1) == 0, pltpu.roll(turned, 1, axis=0), turned)


def spread(row, j):
    return jnp.take_along_axis(jnp.broadcast_to(row, (8, 128)), jnp.full((8, 128), j, jnp.int32), axis=1)


def extras(z2, mv2, scalar):
    lane, sub = iota((16, 128), 1), iota((16, 128), 0)
    first = jnp.sum(jnp.where(lane == 0, z2[pl.ds(0, 16, stride=8), :], 0.0), axis=1, keepdims=True)
    last = jnp.sum(jnp.where(lane == 127, mv2[pl.ds(7, 16, stride=8), :], 0.0), axis=1, keepdims=True)
    row = jnp.where(lane % 32 == sub, first, 0.0) + jnp.where(lane % 32 == sub + N, last, 0.0)
    return jnp.where(iota((1, 128), 1) % 32 == 30, scalar, jnp.sum(row, axis=0, keepdims=True))


def fill(src2, stride, tiles, base, count, onehot, lhs):
    def one(a):
        v = src2[pl.ds(a, 16, stride=stride), :]
        high = v.astype(BF16)
        low = (v - high.astype(F32)).astype(BF16)
        cols = lanes(base + a)
        for n in range(count):
            mask = onehot[n * 16 : (n + 1) * 16, cols]
            lhs[0, n * 16 : (n + 1) * 16, cols] = high * mask
            lhs[1, n * 16 : (n + 1) * 16, cols] = low * mask

    loop(tiles, one)


def spread_sum(lhs, wt, sums, count):
    dims = (((1,), (1,)), ((), ()))
    made = lax.dot_general(lhs[0], wt[...], dims, preferred_element_type=F32) + lax.dot_general(
        lhs[1], wt[...], dims, preferred_element_type=F32
    )
    sums[0, 0:count, :] = made[:, 0:128]
    sums[1, 0:count, :] = made[:, 128:256]


def messages(sums, count, row, out):
    for half in range(2):
        sums[half, pl.ds(N, count, stride=16), :] = jnp.broadcast_to(row, (count, 128))
    group = iota((8, 128), 1) // 32

    def one(hp):
        for half in range(2):
            made = [None] * 4
            for jj in range(4):
                v = sums[half, pl.ds(hp * 32 + jj, 8, stride=4), :]
                for tl in range(4):
                    turn = ((jj - tl) % 4) * 32
                    moved = pltpu.roll(v, turn, axis=1) if turn else v
                    made[tl] = moved if jj == 0 else jnp.where(group == jj, moved, made[tl])
            for tl in range(4):
                out[half * 4 + tl, rows8(hp), :] = made[tl]

    loop(count // 2, one)


def regroup(parts, jj):
    group = iota((8, 128), 1) // 32
    made = None
    for tl in range(4):
        turn = ((tl - jj) % 4) * 32
        moved = pltpu.roll(parts[tl], turn, axis=1) if turn else parts[tl]
        made = moved if tl == 0 else jnp.where(group == tl, moved, made)
    return made


def scalar_of(v):
    keep = (iota(v.shape, 0) % 4 == 3) & (iota(v.shape, 1) % 32 == 30)
    return total(jnp.where(keep, v, 0.0))


def kernel(
    b_ref, slot_row, slot8, cid8, damp_ref, pf_row, ps_row, pf16, ps16, m_any, t_any, blk_any,
    x_out, r_out,
    mb, tb, blk, r2, z2, d2, mv, mvd, e2, jv, x2, near, far, f2, b2, tab, tab2, sums,
    wt_s, oh_s, lhs_s, wt_p, oh_p, lhs_p, lam, out_f, out_b, recv_f, recv_b,
    load_sem, send_sem, recv_sem,
):
    tm = lax.axis_index("tm")
    cl = lax.axis_index("clus")
    flat = tm * 4 + cl
    bar = pltpu.get_barrier_semaphore()
    sweep(lambda t, c: pl.semaphore_signal(bar, 1, device_id=(t, c), device_id_type=MESHID))

    loads = []
    for n, (src, dst) in enumerate(((m_any, mb), (t_any, tb))):
        loads.append(
            [pltpu.make_async_copy(src.at[:, :, pl.ds(a * 128, 128)], dst.at[:, :, a, :], load_sem.at[n, a]) for a in range(8)]
        )
    loads.append([pltpu.make_async_copy(blk_any, blk, load_sem.at[2, 0])])
    for group in loads:
        for copy in group:
            copy.start()

    r2[...] = jnp.zeros_like(r2)
    z2[120:128, :] = jnp.zeros((8, 128), F32)
    mv[120:128, :] = jnp.zeros((8, 128), F32)
    f2[240:256, :] = jnp.zeros((16, 128), F32)
    b2[240:256, :] = jnp.zeros((16, 128), F32)
    for a in range(8):
        r2[pl.ds(a, N, stride=8), :] = b_ref[:, a * 128 : (a + 1) * 128]

    def slots(a):
        index = slot_row[:, lanes(a)]
        wt_s[:, lanes(a)] = jnp.where(iota((256, 128), 0) == index % 256, 1.0, 0.0).astype(BF16)
        oh_s[:, lanes(a)] = jnp.where(iota((64, 128), 0) // 16 == index // 256, 1.0, 0.0).astype(BF16)

    loop(8, slots)

    pos_first = (iota((8, 128), 0) == 0) & (iota((8, 128), 1) == 0)
    pos_last = (iota((8, 128), 0) == 7) & (iota((8, 128), 1) == 127)
    keep_last = jnp.where(pos_last & (flat == 127), 0.0, 1.0)
    keep_first = jnp.where(pos_first & (flat == 0), 0.0, 1.0)
    following, previous = (flat + 1) % 128, (flat + 127) % 128

    def halo(ph, who):
        return recv_f[ph, (who // 4) % 8, pl.ds(((who % 4) * 4 + who // 32) * 4 + 3, 1), :]

    rz = None
    for ph in range(2):
        if ph == 0:
            for copy in loads[0]:
                copy.wait()
        multiply(mb, r2, z2)
        part = total((r2[0:120, :] * z2[0:120, :]).reshape(N, 8, 128))
        if ph == 0:
            for copy in loads[1]:
                copy.wait()
        multiply(tb, z2, mv)
        row = extras(z2, mv, part)
        fill(z2, 8, 8, 0, 4, oh_s, lhs_s)
        spread_sum(lhs_s, wt_s, sums, 64)
        messages(sums, 4, row, out_f.at[ph])
        if ph == 0:
            pl.semaphore_wait(bar, 127)

        def send_f(t, c):
            pltpu.make_async_remote_copy(
                out_f.at[ph, t % 8, rows4(t // 8), :],
                recv_f.at[ph, tm % 8, rows4(cl * 4 + tm // 8), :],
                send_sem.at[ph, 0],
                recv_sem.at[ph, 0],
                device_id=(t, c),
                device_id_type=MESHID,
            ).start()

        sweep(send_f)
        pltpu.make_async_copy(
            out_f.at[ph, tm % 8, rows4(tm // 8), :], recv_f.at[ph, tm % 8, rows4(cl * 4 + tm // 8), :], recv_sem.at[ph, 0]
        ).start()

        if ph == 0:

            def pairs(a):
                for base, ref in ((0, pf_row), (16, ps_row)):
                    index = ref[:, lanes(a)]
                    wt_p[:, lanes(base + a)] = jnp.where(iota((256, 128), 0) == index % 256, 1.0, 0.0).astype(BF16)
                    oh_p[:, lanes(base + a)] = jnp.where(iota((256, 128), 0) // 16 == index // 256, 1.0, 0.0).astype(BF16)

            loop(16, pairs)
            per = jnp.take_along_axis(jnp.broadcast_to(damp_ref[...], (8, 128)), cid8[...], axis=1)
            group = iota((8, 128), 1) // 32
            spare = (iota((4, 128), 0) == 3) & (iota((4, 128), 1) >= 96)
            for tl in range(4):
                wide = None
                for jj in range(4):
                    turn = ((jj - tl) % 4) * 32
                    moved = pltpu.roll(per, turn, axis=1) if turn else per
                    wide = moved if jj == 0 else jnp.where(group == jj, moved, wide)
                for t4 in range(8):
                    th, h = t4 // 2, t4 % 2
                    lam[h * 4 + tl, th * 4 : (th + 1) * 4, :] = jnp.where(spare, 0.0, jnp.broadcast_to(wide[t4 : t4 + 1, :], (4, 128)))
            loads[2][0].wait()

        pltpu.make_async_copy(recv_f.at[ph], recv_f.at[ph], recv_sem.at[ph, 0]).wait()

        def tables(hp):
            for h in range(2):
                parts = [recv_f[ph, h * 4 + tl, rows8(hp), :] for tl in range(4)]
                for jj in range(4):
                    tab[jj, h, rows8(hp), :] = regroup(parts, jj)

        loop(8, tables)
        rz_new = scalar_of(tab[3, 0]) + scalar_of(tab[3, 1])
        nxt, prv = halo(ph, following), halo(ph, previous)
        if ph == 0:
            rz = rz_new
            d2[...] = z2[...]
            mvd[...] = mv[...]
        else:
            beta = rz_new / rz
            rz = rz_new
            nxt = nxt + beta * halo(0, following)
            prv = prv + beta * halo(0, previous)
            d2[...] = z2[...] + beta * d2[...]
            mvd[...] = mv[...] + beta * mvd[...]

        def residuals(j):
            v = jnp.where(pos_last, spread(nxt, j + 96), after(d2[rows8(j), :]))
            e2[rows8(j), :] = (v - mvd[rows8(j), :]) * keep_last

        loop(N, residuals)

        for index16, field in ((pf16, near), (ps16, far)):
            index = [index16[pv * 8 : (pv + 1) * 8, :] for pv in range(2)]
            high = [v // 128 for v in index]
            low = [v % 128 for v in index]

            def look(hi, carry):
                carry = list(carry)
                for h in range(2):
                    here = [v == hi * 2 + h for v in high]
                    for j in range(N):
                        src = jnp.broadcast_to(tab[j % 4, h, pl.ds(hi * 4 + j // 4, 1), :], (8, 128))
                        for pv in range(2):
                            k = j * 2 + pv
                            carry[k] = jnp.where(here[pv], jnp.take_along_axis(src, low[pv], axis=1), carry[k])
                return tuple(carry)

            found = lax.fori_loop(0, 16, look, tuple(jnp.zeros((8, 128), F32) for _ in range(30)))
            for j in range(N):
                for pv in range(2):
                    v = found[j * 2 + pv]
                    if ph == 1:
                        v = v + beta * field[j, pv * 8 : (pv + 1) * 8, :]
                    field[j, pv * 8 : (pv + 1) * 8, :] = v

        def forward(i):
            f2[rows16(i), :] = near[i] - jnp.sum(blk[i] * far[...], axis=0)

        loop(N, forward)

        def backward(j):
            b2[rows16(j), :] = -jnp.sum(blk[:, j] * f2[0:240, :].reshape(N, 16, 128), axis=0)

        loop(N, backward)
        own = recv_f[ph, :, rows16(cl), :]
        if ph == 1:
            own = own + beta * recv_f[0, :, rows16(cl), :]
        damped = own * lam[...]
        errors = e2[0:120, :].reshape(N, 8, 128)
        part = total((f2[0:240, :] * f2[0:240, :]).reshape(N, 16, 128)) + total(errors * errors) + total(damped * own)
        fill(f2, 16, 16, 0, 16, oh_p, lhs_p)
        fill(b2, 16, 16, 16, 16, oh_p, lhs_p)
        spread_sum(lhs_p, wt_p, sums, 256)
        row = jnp.where(iota((1, 128), 1) % 32 == 30, part, 0.0)
        messages(sums, 16, row, out_b.at[ph])
        out_b[ph, :, rows16(cl), :] = out_b[ph, :, rows16(cl), :] + damped

        def send_b(t, c):
            pltpu.make_async_remote_copy(
                out_b.at[ph, t % 8, rows4(c * 4 + t // 8), :],
                recv_b.at[ph, tm % 4, cl, rows4(tm // 4), :],
                send_sem.at[ph, 1],
                recv_sem.at[ph, 1],
                device_id=(t, c),
                device_id_type=MESHID,
            ).start()

        sweep(send_b)
        pltpu.make_async_copy(
            out_b.at[ph, tm % 8, rows4(cl * 4 + tm // 8), :], recv_b.at[ph, tm % 4, cl, rows4(tm // 4), :], recv_sem.at[ph, 1]
        ).start()

        errors = e2[0:120, :].reshape(N, 8, 128)

        def inertial(j):
            edge = (d2[rows8(j), :] - spread(prv, j + 96 + N)) * keep_first
            shifted = jnp.where(pos_first, edge, before(e2[rows8(j), :]))
            jv[rows8(j), :] = shifted - jnp.sum(tb[:, j] * errors, axis=0)

        loop(N, inertial)

        pltpu.make_async_copy(recv_b.at[ph], recv_b.at[ph], recv_sem.at[ph, 1]).wait()

        def tables2(gp):
            parts = [jnp.sum(recv_b[ph, gl, :, rows8(gp), :], axis=0) for gl in range(4)]
            for jj in range(4):
                tab2[jj, rows8(gp), :] = regroup(parts, jj)

        loop(4, tables2)
        alpha = rz / scalar_of(tab2[3])
        high, low = slot8[...] // 128, slot8[...] % 128
        for j in range(N):
            v = jv[j * 8 : (j + 1) * 8, :]
            found = jnp.zeros((8, 128), F32)
            for g4 in range(8):
                src = jnp.broadcast_to(tab2[j % 4, g4 * 4 + j // 4 : g4 * 4 + j // 4 + 1, :], (8, 128))
                found = jnp.where(high == g4, jnp.take_along_axis(src, low, axis=1), found)
            at = slice(j * 8, (j + 1) * 8)
            step = alpha * d2[at, :]
            x2[at, :] = step if ph == 0 else x2[at, :] + step
            r2[at, :] = r2[at, :] - alpha * (v + found)

    for a in range(8):
        x_out[:, a * 128 : (a + 1) * 128] = x2[pl.ds(a, 16, stride=8), :][:N, :]
        r_out[:, a * 128 : (a + 1) * 128] = r2[pl.ds(a, 16, stride=8), :][:N, :]
    for ph in range(2):
        for way in range(2):
            sent = sums.at[:, pl.ds(0, 254), :]
            pltpu.make_async_copy(sent, sent, send_sem.at[ph, way]).wait()


def on_device(right_side, transition, precond, slot_of, cluster_id, damping, pair_first, pair_second, pair_blocks):
    vm = pl.BlockSpec(memory_space=pltpu.VMEM)
    anywhere = pl.BlockSpec(memory_space=pl.ANY)
    field = pltpu.VMEM((128, 128), F32)
    call = pl.pallas_call(
        kernel,
        out_shape=(jax.ShapeDtypeStruct((N, 1024), F32),) * 2,
        in_specs=[vm] * 9 + [anywhere] * 3,
        out_specs=(vm, vm),
        scratch_shapes=[
            pltpu.VMEM((N, N, 8, 128), F32),
            pltpu.VMEM((N, N, 8, 128), F32),
            pltpu.VMEM((N, N, 16, 128), F32),
            field, field, field, field, field, field, field, field,
            pltpu.VMEM((N, 16, 128), F32),
            pltpu.VMEM((N, 16, 128), F32),
            pltpu.VMEM((256, 128), F32),
            pltpu.VMEM((256, 128), F32),
            pltpu.VMEM((4, 2, 64, 128), F32),
            pltpu.VMEM((4, 32, 128), F32),
            pltpu.VMEM((2, 256, 128), F32),
            pltpu.VMEM((256, 1024), BF16),
            pltpu.VMEM((64, 1024), BF16),
            pltpu.VMEM((2, 64, 1024), BF16),
            pltpu.VMEM((256, 4096), BF16),
            pltpu.VMEM((256, 4096), BF16),
            pltpu.VMEM((2, 256, 4096), BF16),
            pltpu.VMEM((8, 16, 128), F32),
            pltpu.VMEM((2, 8, 16, 128), F32),
            pltpu.VMEM((2, 8, 64, 128), F32),
            pltpu.VMEM((2, 8, 64, 128), F32),
            pltpu.VMEM((2, 4, 4, 32, 128), F32),
            pltpu.SemaphoreType.DMA((3, 8)),
            pltpu.SemaphoreType.DMA((2, 2)),
            pltpu.SemaphoreType.DMA((2, 2)),
        ],
        compiler_params=pltpu.CompilerParams(collective_id=0, has_side_effects=True, vmem_limit_bytes=60 * 1024 * 1024),
    )
    return call(
        right_side,
        slot_of.reshape(1, 1024),
        slot_of.reshape(8, 128),
        cluster_id.reshape(8, 128),
        jnp.pad(damping, ((0, 0), (0, 64))),
        pair_first.reshape(1, 2048),
        pair_second.reshape(1, 2048),
        pair_first.reshape(16, 128),
        pair_second.reshape(16, 128),
        precond,
        transition,
        pair_blocks.reshape(N, N, 16, 128),
    )


def solution(mesh):
    placed = (
        P(None, ("tm", "clus")),
        P(None, None, ("tm", "clus")),
        P(None, None, ("tm", "clus")),
        P(("tm", "clus")),
        P("tm", "clus"),
        P("tm", None),
        P("tm", "clus"),
        P("tm", "clus"),
        P(None, None, "tm", "clus"),
    )
    return jax.shard_map(
        on_device,
        mesh=mesh,
        in_specs=placed,
        out_specs=(P(None, ("tm", "clus")), P(None, ("tm", "clus"))),
        check_vma=False,
    )
```

time: 628 us -> 74.1 us (0.12); the launches traced: 621 us -> 73.9 us
  blocking collectives: 242 us -> 0 us
  local copies, waits for them, and re-layouts: 160 us -> 4.12 us
  other arithmetic: 130 us -> 0 us
  Pallas kernels: 0 us -> 69.1 us
  starting transfers between devices: 37.7 us -> 0 us
  waiting for transfers between devices: 32 us -> 0 us
  between operations: 20.2 us -> 0.64 us
    psum x3 -> x0, blocking collectives: 189 us -> none  [the longest x2 126 us: precond_dot(): return lax.psum(jnp.sum(residual * scaled), ('tm', 'clus'))]
    pallas_call x0 -> x1, Pallas kernels: none -> 69.1 us  [on_device(): call(right_side, slot_of.reshape(1, 1024), slot_of.reshape(8, 128), clust...]
    scatter-add x5 -> x0, other arithmetic: 61.1 us -> none  [the longest x4 53.5 us: add_columns(): return jax.ops.segment_sum(values.T, index, num_segments=count).T]
    slice x20 -> x0, local copies, waits for them, and re-layouts: 56.7 us -> none  [the longest x7 33.6 us: batched(): total = blocks[:, 0, :] * field[0][None, :]]
    gather x8 -> x0, local copies, waits for them, and re-layouts: 44.2 us -> none  [take_columns(): return jnp.take(field.T, index, axis=0).T]
    unnamed x238 -> x2, local copies, waits for them, and re-layouts: 45.6 us -> 2.95 us
    all_gather x2 -> x0, blocking collectives: 41.7 us -> none  [on_device(): grouped = lax.all_gather(own, 'clus', axis=1, tiled=True)]
    sub x6 -> x0, other arithmetic: 28.7 us -> none  [the longest x2 20.3 us: on_device(): errors = near - batched(blocks, far)]
  transfers between devices with their start and end apart: 9 -> 0, of which waited for: 5 -> 0; matrix products, arithmetic and copies ran while one was open for 23% -> 0% of each run, Pallas kernels for 0% -> 0%
where the time goes in v1:
time: 74.1 us; the launch traced here: 73.9 us
  Pallas kernels  69.1 us (93%)
  local copies, waits for them, and re-layouts  4.12 us (6%)
    pallas_call x1, Pallas kernels, on_device(): call(right_side, slot_of.reshape(1, 1024), slot_of.reshape(8, 128), clust...  69.1 us
    unnamed x2, local copies, waits for them, and re-layouts  2.95 us

profile of v1, /device:TPU:1, one launch (start us, length us, event | category | flops | bytes accessed | tf_op | source)
XLA Modules:
  0.0 73.9 jit_solution(5822846036388384374)
XLA Ops:
  0.6 1.2 %pad.4.damp_ref = f32[1,128]{1,0:T(1,128)} pad(f32[1,64]{1,0:T(1,128)} %param.14, f32[]{:T(128)} %constant.2.clone.1), padding=0_0x0_64 | pad | bytes 772 | tf_op jit(solution)/shard_map/jit(_pad)/pad | solution.py:434
  1.8 69.1 %shard_map.104 = (f32[15,1024]{1,0:T(8,128)}, f32[15,1024]{1,0:T(8,128)}) custom-call(f32[15,1024]{1,0:T(8,128)} %b_ref.1, s32[1,1024]{1,0:T(1,128)} %bitcast.9, s32[8,128]{1,0:T(8,128)} %bitcast.10, s32[8,128]{1,0:T(8,128)} %bitcast.11, f32[1,128]{1,0:T(1,128)} %pad.4.damp_ref, s32[1,2048]{1,0:T(1,128)} %pf_row.1, s32[1,2048]{1,0:T(1,128)} %ps_row.1, ...), custom_call_target="tpu_custom_call" | custom-call | tf_op jit(solution)/shard_map/pallas_call | solution.py:429
  70.9 1.5 %copy.13 = f32[15,1024]{1,0:T(8,128)} copy(f32[15,1024]{1,0:T(8,128)} %get-tuple-element.4) | data formatting | bytes 122880
  72.4 1.5 %copy.14 = f32[15,1024]{1,0:T(8,128)} copy(f32[15,1024]{1,0:T(8,128)} %get-tuple-element.5) | data formatting | bytes 122880

commit v2 on v1

v2 whole, which is shorter than its diff:
```python
import jax
import jax.numpy as jnp
from jax import lax
from jax.experimental import pallas as pl
from jax.experimental.pallas import tpu as pltpu
from jax.sharding import PartitionSpec as P

MESHID = pl.DeviceIdType.MESH
F32 = jnp.float32
BF16 = jnp.bfloat16
N = 15


def hops(d):
    return min(d, 4 - d)


OFFSETS = sorted(
    ((z, y, c, x) for z in range(4) for y in range(4) for c in range(2) for x in range(4) if z or y or c or x),
    key=lambda o: -hops(o[0]) - hops(o[1]) - hops(o[3]),
)


def place():
    tm = lax.axis_index("tm")
    return lax.div(tm, 8), lax.rem(lax.div(tm, 2), 4), lax.rem(tm, 2), lax.axis_index("clus")


def sweep(action):
    sizes = (4, 4, 2, 4)
    turned = [[lax.rem(at + d, n) for d in range(n)] for at, n in zip(place(), sizes)]
    for offset in OFFSETS:
        action(*(turned[k][d] for k, d in enumerate(offset)))


def device(z, y, core, x):
    return (z * 8 + y * 2 + core, x)


def iota(shape, axis):
    return lax.broadcasted_iota(jnp.int32, shape, axis)


def total(v):
    while v.ndim > 2:
        v = jnp.sum(v, axis=0)
    return jnp.sum(v, axis=(0, 1), keepdims=True)


def loop(n, body, unroll=1):
    def step(i, c):
        body(i)
        return c

    lax.fori_loop(0, n, step, 0, unroll=unroll)


def rows8(i):
    return pl.ds(pl.multiple_of(i * 8, 8), 8)


def rows16(i):
    return pl.ds(pl.multiple_of(i * 16, 16), 16)


def rows4(i):
    return pl.ds(pl.multiple_of(i * 4, 4), 4)


def lanes(i):
    return pl.ds(pl.multiple_of(i * 128, 128), 128)


def multiply(blocks, src, dst):
    field = src[0:N]

    def one(i):
        dst[rows8(i), :] = jnp.sum(blocks[i] * field, axis=0)

    loop(N, one)


def after(v):
    turned = pltpu.roll(v, 127, axis=1)
    return jnp.where(iota((8, 128), 1) == 127, pltpu.roll(turned, 7, axis=0), turned)


def before(v):
    turned = pltpu.roll(v, 1, axis=1)
    return jnp.where(iota((8, 128), 1) == 0, pltpu.roll(turned, 1, axis=0), turned)


def spread(row, j):
    return jnp.take_along_axis(jnp.broadcast_to(row, (8, 128)), jnp.full((8, 128), j, jnp.int32), axis=1)


def extras(z2, mv2, scalar):
    lane, sub = iota((16, 128), 1), iota((16, 128), 0)
    first = jnp.sum(jnp.where(lane == 0, z2[pl.ds(0, 16, stride=8), :], 0.0), axis=1, keepdims=True)
    last = jnp.sum(jnp.where(lane == 127, mv2[pl.ds(7, 16, stride=8), :], 0.0), axis=1, keepdims=True)
    row = jnp.where(lane % 32 == sub, first, 0.0) + jnp.where(lane % 32 == sub + N, last, 0.0)
    return jnp.where(iota((1, 128), 1) % 32 == 30, scalar, jnp.sum(row, axis=0, keepdims=True))


def fill(src2, stride, tiles, base, count, onehot, lhs):
    def one(a):
        v = src2[pl.ds(a, 16, stride=stride), :]
        high = v.astype(BF16)
        low = (v - high.astype(F32)).astype(BF16)
        cols = lanes(base + a)
        for n in range(count):
            mask = onehot[n * 16 : (n + 1) * 16, cols]
            lhs[n * 16 : (n + 1) * 16, cols] = high * mask
            lhs[(count + n) * 16 : (count + n + 1) * 16, cols] = low * mask

    loop(tiles, one, 2)


def spread_sum(lhs, wt, sums, count):
    made = lax.dot_general(lhs[...], wt[...], (((1,), (1,)), ((), ())), preferred_element_type=F32)
    made = made[0:count] + made[count:]
    sums[0, 0:count, :] = made[:, 0:128]
    sums[1, 0:count, :] = made[:, 128:256]


def messages(sums, count, row, out):
    for half in range(2):
        sums[half, pl.ds(N, count, stride=16), :] = jnp.broadcast_to(row, (count, 128))
    group = iota((8, 128), 1) // 32

    def one(hp):
        for half in range(2):
            made = [None] * 4
            for jj in range(4):
                v = sums[half, pl.ds(hp * 32 + jj, 8, stride=4), :]
                for tl in range(4):
                    turn = ((jj - tl) % 4) * 32
                    moved = pltpu.roll(v, turn, axis=1) if turn else v
                    made[tl] = moved if jj == 0 else jnp.where(group == jj, moved, made[tl])
            for tl in range(4):
                out[half * 4 + tl, rows8(hp), :] = made[tl]

    loop(count // 2, one, 2)


def regroup(parts, jj):
    group = iota((8, 128), 1) // 32
    made = None
    for tl in range(4):
        turn = ((tl - jj) % 4) * 32
        moved = pltpu.roll(parts[tl], turn, axis=1) if turn else parts[tl]
        made = moved if tl == 0 else jnp.where(group == tl, moved, made)
    return made


def scalar_of(v):
    keep = (iota(v.shape, 0) % 4 == 3) & (iota(v.shape, 1) % 32 == 30)
    return total(jnp.where(keep, v, 0.0))


def kernel(
    b_any, slot_any, slot8_any, cid8_any, damp_any, pf_any, ps_any, pf16_any, ps16_any, m_any, t_any, blk_any,
    out,
    slot_row, slot8, cid8, damp, pf_row, ps_row, pf16, ps16,
    mb, tb, blk, r3, z2, d2, mv, ez, e2, jv, near, far, f2, b2, tab, tab2, sums,
    wt_s, oh_s, lhs_s, wt_p, oh_p, lhs_p, lam, out_f, out_b, recv_f, recv_b,
    load_sem, send_sem, recv_sem,
):
    tm = lax.axis_index("tm")
    cl = lax.axis_index("clus")
    flat = tm * 4 + cl
    my_z, my_y, my_core, my_x = place()
    my_tl = my_y * 2 + my_core
    bar = pltpu.get_barrier_semaphore()
    sweep(lambda *who: pl.semaphore_signal(bar, 1, device_id=device(*who), device_id_type=MESHID))

    def spread_load(n, src, dst):
        if len(dst.shape) == 3:
            return [
                pltpu.make_async_copy(src.at[:, pl.ds(a * 128, 128)], dst.at[pl.ds(0, N), a, :], load_sem.at[n, a]) for a in range(8)
            ]
        return [pltpu.make_async_copy(src.at[:, :, pl.ds(a * 128, 128)], dst.at[:, :, a, :], load_sem.at[n, a]) for a in range(8)]

    small = ((slot_any, slot_row), (slot8_any, slot8), (cid8_any, cid8), (damp_any, damp))
    small += ((pf_any, pf_row), (ps_any, ps_row), (pf16_any, pf16), (ps16_any, ps16))
    load_small = [pltpu.make_async_copy(src, dst, load_sem.at[3, n]) for n, (src, dst) in enumerate(small)]
    load_r, load_m, load_t = spread_load(0, b_any, r3), spread_load(1, m_any, mb), spread_load(2, t_any, tb)
    load_blk = pltpu.make_async_copy(blk_any, blk, load_sem.at[4, 0])
    for copy in load_small[:1] + load_r + load_m + load_t + load_small[1:]:
        copy.start()

    z2[120:128, :] = jnp.zeros((8, 128), F32)
    mv[120:128, :] = jnp.zeros((8, 128), F32)
    f2[240:256, :] = jnp.zeros((16, 128), F32)
    b2[240:256, :] = jnp.zeros((16, 128), F32)
    load_small[0].wait()

    def slots(a):
        index = slot_row[:, lanes(a)]
        wt_s[:, lanes(a)] = jnp.where(iota((256, 128), 0) == index % 256, 1.0, 0.0).astype(BF16)
        oh_s[:, lanes(a)] = jnp.where(iota((64, 128), 0) // 16 == index // 256, 1.0, 0.0).astype(BF16)

    loop(8, slots, 2)
    for copy in load_r:
        copy.wait()

    pos_first = (iota((8, 128), 0) == 0) & (iota((8, 128), 1) == 0)
    pos_last = (iota((8, 128), 0) == 7) & (iota((8, 128), 1) == 127)
    keep_last = jnp.where(pos_last & (flat == 127), 0.0, 1.0)
    keep_first = jnp.where(pos_first & (flat == 0), 0.0, 1.0)
    following, previous = (flat + 1) % 128, (flat + 127) % 128

    def halo(ph, who):
        return recv_f[ph, (who // 4) % 8, pl.ds(((who % 4) * 4 + who // 32) * 4 + 3, 1), :]

    rz = None
    for ph in range(2):
        if ph == 0:
            for copy in load_m:
                copy.wait()
            load_blk.start()
        multiply(mb, r3, z2)
        z3 = z2[0:120, :].reshape(N, 8, 128)
        part = total(r3[0:N] * z3)
        if ph == 0:
            for copy in load_t:
                copy.wait()
        multiply(tb, z3, mv)
        row = extras(z2, mv, part)
        fill(z2, 8, 8, 0, 4, oh_s, lhs_s)
        spread_sum(lhs_s, wt_s, sums, 64)
        messages(sums, 4, row, out_f.at[ph])
        if ph == 0:
            pl.semaphore_wait(bar, 127)

        def send_f(z, y, core, x):
            pltpu.make_async_remote_copy(
                out_f.at[ph, y * 2 + core, rows4(z), :],
                recv_f.at[ph, my_tl, rows4(my_x * 4 + my_z), :],
                send_sem.at[ph, 0],
                recv_sem.at[ph, 0],
                device_id=device(z, y, core, x),
                device_id_type=MESHID,
            ).start()

        sweep(send_f)
        pltpu.make_async_copy(
            out_f.at[ph, my_tl, rows4(my_z), :], recv_f.at[ph, my_tl, rows4(my_x * 4 + my_z), :], recv_sem.at[ph, 0]
        ).start()

        for j in range(N):
            at = slice(j * 8, (j + 1) * 8)
            ez[at, :] = jnp.where(pos_last, 0.0, after(z2[at, :])) - mv[at, :]
        if ph == 0:
            for copy in load_small[1:]:
                copy.wait()

            def pairs(a):
                for base, ref in ((0, pf_row), (16, ps_row)):
                    index = ref[:, lanes(a)]
                    wt_p[:, lanes(base + a)] = jnp.where(iota((256, 128), 0) == index % 256, 1.0, 0.0).astype(BF16)
                    oh_p[:, lanes(base + a)] = jnp.where(iota((256, 128), 0) // 16 == index // 256, 1.0, 0.0).astype(BF16)

            loop(16, pairs, 2)
            per = jnp.take_along_axis(jnp.broadcast_to(jnp.concatenate([damp[...]] * 2, axis=1), (8, 128)), cid8[...], axis=1)
            group = iota((8, 128), 1) // 32
            spare = (iota((4, 128), 0) == 3) & (iota((4, 128), 1) >= 96)
            for tl in range(4):
                wide = None
                for jj in range(4):
                    turn = ((jj - tl) % 4) * 32
                    moved = pltpu.roll(per, turn, axis=1) if turn else per
                    wide = moved if jj == 0 else jnp.where(group == jj, moved, wide)
                for t4 in range(8):
                    th, h = t4 // 2, t4 % 2
                    lam[h * 4 + tl, th * 4 : (th + 1) * 4, :] = jnp.where(spare, 0.0, jnp.broadcast_to(wide[t4 : t4 + 1, :], (4, 128)))
            load_blk.wait()

        pltpu.make_async_copy(recv_f.at[ph], recv_f.at[ph], recv_sem.at[ph, 0]).wait()

        def tables(hp):
            for h in range(2):
                parts = [recv_f[ph, h * 4 + tl, rows8(hp), :] for tl in range(4)]
                for jj in range(4):
                    tab[jj, h, rows8(hp), :] = regroup(parts, jj)

        loop(8, tables, 2)
        rz_new = scalar_of(tab[3, 0]) + scalar_of(tab[3, 1])
        nxt, prv = halo(ph, following), halo(ph, previous)
        if ph == 0:
            rz = rz_new
            d2[...] = z2[...]
        else:
            beta = rz_new / rz
            rz = rz_new
            prv = prv + beta * halo(0, previous)
            d2[...] = z2[...] + beta * d2[...]
        part = jnp.zeros((8, 128), F32)
        for j in range(N):
            at = slice(j * 8, (j + 1) * 8)
            v = (ez[at, :] + jnp.where(pos_last, spread(nxt, j + 96), 0.0)) * keep_last
            if ph == 1:
                v = v + beta * e2[at, :]
            e2[at, :] = v
            part = part + v * v
        part = total(part)

        for index16, field in ((pf16, near), (ps16, far)):
            index = [index16[pv * 8 : (pv + 1) * 8, :] for pv in range(2)]
            high = [v // 128 for v in index]
            low = [v % 128 for v in index]

            def look(quad, carry):
                carry = list(carry)
                for low_hi in range(4):
                    for h in range(2):
                        here = [v == quad * 8 + low_hi * 2 + h for v in high]
                        for j in range(N):
                            row = tab[j % 4, h, pl.ds(quad * 16 + low_hi * 4 + j // 4, 1), :]
                            src = jnp.broadcast_to(row, (8, 128))
                            for pv in range(2):
                                k = j * 2 + pv
                                carry[k] = jnp.where(here[pv], jnp.take_along_axis(src, low[pv], axis=1), carry[k])
                return tuple(carry)

            found = lax.fori_loop(0, 4, look, tuple(jnp.zeros((8, 128), F32) for _ in range(30)))
            for j in range(N):
                for pv in range(2):
                    v = found[j * 2 + pv]
                    if ph == 1:
                        v = v + beta * field[j, pv * 8 : (pv + 1) * 8, :]
                    field[j, pv * 8 : (pv + 1) * 8, :] = v

        def forward(i):
            f2[rows16(i), :] = near[i] - jnp.sum(blk[i] * far[...], axis=0)

        loop(N, forward, 3)

        def backward(j):
            b2[rows16(j), :] = -jnp.sum(blk[:, j] * f2[0:240, :].reshape(N, 16, 128), axis=0)

        loop(N, backward, 3)
        own = recv_f[ph, :, rows16(cl), :]
        if ph == 1:
            own = own + beta * recv_f[0, :, rows16(cl), :]
        damped = own * lam[...]
        part = part + total((f2[0:240, :] * f2[0:240, :]).reshape(N, 16, 128)) + total(damped * own)
        fill(f2, 16, 16, 0, 16, oh_p, lhs_p)
        fill(b2, 16, 16, 16, 16, oh_p, lhs_p)
        spread_sum(lhs_p, wt_p, sums, 256)
        row = jnp.where(iota((1, 128), 1) % 32 == 30, part, 0.0)
        messages(sums, 16, row, out_b.at[ph])
        out_b[ph, :, rows16(cl), :] = out_b[ph, :, rows16(cl), :] + damped

        def send_b(z, y, core, x):
            pltpu.make_async_remote_copy(
                out_b.at[ph, y * 2 + core, rows4(x * 4 + z), :],
                recv_b.at[ph, lax.rem(my_tl, 4), my_x, rows4(my_z * 2 + lax.div(my_tl, 4)), :],
                send_sem.at[ph, 1],
                recv_sem.at[ph, 1],
                device_id=device(z, y, core, x),
                device_id_type=MESHID,
            ).start()

        sweep(send_b)
        pltpu.make_async_copy(
            out_b.at[ph, my_tl, rows4(my_x * 4 + my_z), :],
            recv_b.at[ph, lax.rem(my_tl, 4), my_x, rows4(my_z * 2 + lax.div(my_tl, 4)), :],
            recv_sem.at[ph, 1],
        ).start()

        errors = e2[0:120, :].reshape(N, 8, 128)

        def inertial(j):
            edge = (d2[rows8(j), :] - spread(prv, j + 96 + N)) * keep_first
            shifted = jnp.where(pos_first, edge, before(e2[rows8(j), :]))
            jv[rows8(j), :] = shifted - jnp.sum(tb[:, j] * errors, axis=0)

        loop(N, inertial, 3)

        pltpu.make_async_copy(recv_b.at[ph], recv_b.at[ph], recv_sem.at[ph, 1]).wait()

        def tables2(gp):
            parts = [jnp.sum(recv_b[ph, gl, :, rows8(gp), :], axis=0) for gl in range(4)]
            for jj in range(4):
                tab2[jj, rows8(gp), :] = regroup(parts, jj)

        loop(4, tables2, 4)
        alpha = rz / scalar_of(tab2[3])
        high, low = slot8[...] // 128, slot8[...] % 128
        for j in range(N):
            v = jv[j * 8 : (j + 1) * 8, :]
            found = jnp.zeros((8, 128), F32)
            for g4 in range(8):
                src = jnp.broadcast_to(tab2[j % 4, g4 * 4 + j // 4 : g4 * 4 + j // 4 + 1, :], (8, 128))
                found = jnp.where(high == g4, jnp.take_along_axis(src, low, axis=1), found)
            at = slice(j * 8, (j + 1) * 8)
            step = alpha * d2[at, :]
            out[0, j] = step if ph == 0 else out[0, j] + step
            r3[j] = r3[j] - alpha * (v + found)

    out[1] = r3[...]
    for ph in range(2):
        for way in range(2):
            sent = sums.at[:, pl.ds(0, 254), :]
            pltpu.make_async_copy(sent, sent, send_sem.at[ph, way]).wait()


def finish(both, x_out, r_out, sem):
    copies = [
        pltpu.make_async_copy(both.at[n, pl.ds(0, N), a, :], dst.at[:, pl.ds(a * 128, 128)], sem.at[n, a])
        for n, dst in enumerate((x_out, r_out))
        for a in range(8)
    ]
    for copy in copies:
        copy.start()
    for copy in copies:
        copy.wait()


def on_device(right_side, transition, precond, slot_of, cluster_id, damping, pair_first, pair_second, pair_blocks):
    vm = pl.BlockSpec(memory_space=pltpu.VMEM)
    anywhere = pl.BlockSpec(memory_space=pl.ANY)
    field = pltpu.VMEM((128, 128), F32)
    whole = jnp.int32
    both = pl.pallas_call(
        kernel,
        out_shape=jax.ShapeDtypeStruct((2, 16, 8, 128), F32),
        in_specs=[anywhere] * 12,
        out_specs=vm,
        scratch_shapes=[
            pltpu.VMEM((1, 1024), whole), pltpu.VMEM((8, 128), whole), pltpu.VMEM((8, 128), whole), pltpu.VMEM((1, 64), F32),
            pltpu.VMEM((1, 2048), whole), pltpu.VMEM((1, 2048), whole), pltpu.VMEM((16, 128), whole), pltpu.VMEM((16, 128), whole),
            pltpu.VMEM((N, N, 8, 128), F32),
            pltpu.VMEM((N, N, 8, 128), F32),
            pltpu.VMEM((N, N, 16, 128), F32),
            pltpu.VMEM((16, 8, 128), F32),
            field, field, field, field, field, field,
            pltpu.VMEM((N, 16, 128), F32),
            pltpu.VMEM((N, 16, 128), F32),
            pltpu.VMEM((256, 128), F32),
            pltpu.VMEM((256, 128), F32),
            pltpu.VMEM((4, 2, 64, 128), F32),
            pltpu.VMEM((4, 32, 128), F32),
            pltpu.VMEM((2, 256, 128), F32),
            pltpu.VMEM((256, 1024), BF16),
            pltpu.VMEM((64, 1024), BF16),
            pltpu.VMEM((128, 1024), BF16),
            pltpu.VMEM((256, 4096), BF16),
            pltpu.VMEM((256, 4096), BF16),
            pltpu.VMEM((512, 4096), BF16),
            pltpu.VMEM((8, 16, 128), F32),
            pltpu.VMEM((2, 8, 16, 128), F32),
            pltpu.VMEM((2, 8, 64, 128), F32),
            pltpu.VMEM((2, 8, 64, 128), F32),
            pltpu.VMEM((2, 4, 4, 32, 128), F32),
            pltpu.SemaphoreType.DMA((5, 8)),
            pltpu.SemaphoreType.DMA((2, 2)),
            pltpu.SemaphoreType.DMA((2, 2)),
        ],
        compiler_params=pltpu.CompilerParams(collective_id=0, has_side_effects=True, vmem_limit_bytes=60 * 1024 * 1024),
    )(
        right_side,
        slot_of.reshape(1, 1024),
        slot_of.reshape(8, 128),
        cluster_id.reshape(8, 128),
        damping,
        pair_first.reshape(1, 2048),
        pair_second.reshape(1, 2048),
        pair_first.reshape(16, 128),
        pair_second.reshape(16, 128),
        precond,
        transition,
        pair_blocks.reshape(N, N, 16, 128),
    )
    return pl.pallas_call(
        finish,
        out_shape=(jax.ShapeDtypeStruct((N, 1024), F32),) * 2,
        in_specs=[vm],
        out_specs=(anywhere, anywhere),
        scratch_shapes=[pltpu.SemaphoreType.DMA((2, 8))],
    )(both)


def solution(mesh):
    placed = (
        P(None, ("tm", "clus")),
        P(None, None, ("tm", "clus")),
        P(None, None, ("tm", "clus")),
        P(("tm", "clus")),
        P("tm", "clus"),
        P("tm", None),
        P("tm", "clus"),
        P("tm", "clus"),
        P(None, None, "tm", "clus"),
    )
    return jax.shard_map(
        on_device,
        mesh=mesh,
        in_specs=placed,
        out_specs=(P(None, ("tm", "clus")), P(None, ("tm", "clus"))),
        check_vma=False,
    )
```

time: 74.1 us -> 59.7 us (0.81)
  Pallas kernels: 69.1 us -> 58.9 us
  local copies, waits for them, and re-layouts: 4.12 us -> 0 us
    pallas_call x1 -> x2, Pallas kernels: 69.1 us -> 58.9 us  [the longest x1 57.1 us: on_device(): pl.pallas_call(kernel, out_shape=jax.ShapeDtypeStruct((2, 16, 8, 128), F3...]
    unnamed x2 -> x0, local copies, waits for them, and re-layouts: 2.95 us -> none
    pad x1 -> x0, local copies, waits for them, and re-layouts: 1.17 us -> none  [on_device(): jnp.pad(damping, ((0, 0), (0, 64)))]
where the time goes in v2:
time: 59.7 us; the launch traced here: 59.5 us
  Pallas kernels  58.9 us (99%)
  between operations  0.64 us (1%)
    pallas_call x1, Pallas kernels, on_device(): pl.pallas_call(kernel, out_shape=jax.ShapeDtypeStruct((2, 16, 8, 128), F3...  57.1 us
    pallas_call x1, Pallas kernels, on_device(): pl.pallas_call(finish, out_shape=(jax.ShapeDtypeStruct((N, 1024), F32),)...  1.75 us

profile of v2, /device:TPU:1, one launch (start us, length us, event | category | flops | bytes accessed | tf_op | source)
XLA Modules:
  0.0 59.5 jit_solution(12177783795376824372)
XLA Ops:
  0.6 57.1 %shard_map.104.both = f32[2,16,8,128]{3,2,1,0:T(8,128)} custom-call(f32[15,1024]{1,0:T(8,128)} %b_any.1, s32[1,1024]{1,0:T(1,128)} %bitcast.9, s32[8,128]{1,0:T(8,128)} %bitcast.10, s32[8,128]{1,0:T(8,128)} %bitcast.11, f32[1,64]{1,0:T(1,128)} %damp_any.1, s32[1,2048]{1,0:T(1,128)} %pf_any.1, s32[1,2048]{1,0:T(1,128)} %ps_any.1, s32[16,128]{1,0:T(8,128)} %bitcast.7, ...), custom_call_target="tpu_custom_call" | custom-call | tf_op jit(solution)/shard_map/pallas_call | solution.py:426
  57.8 1.8 %shard_map.105 = (f32[15,1024]{1,0:T(8,128)}, f32[15,1024]{1,0:T(8,128)}) custom-call(f32[2,16,8,128]{3,2,1,0:T(8,128)} %shard_map.104.both), custom_call_target="tpu_custom_call" | custom-call | tf_op jit(solution)/shard_map/pallas_call | solution.py:476

commit v3 on v2

--- a/solution.py
+++ b/solution.py
@@ -21,16 +21,20 @@
 )
 
 
+TURNS = ((2, 1, 3, 0),)
+
+
 def place():
     tm = lax.axis_index("tm")
     return lax.div(tm, 8), lax.rem(lax.div(tm, 2), 4), lax.rem(tm, 2), lax.axis_index("clus")
 
 
-def sweep(action):
+def sweep(action, turns=(0, 1, 2, 3)):
     sizes = (4, 4, 2, 4)
     turned = [[lax.rem(at + d, n) for d in range(n)] for at, n in zip(place(), sizes)]
     for offset in OFFSETS:
-        action(*(turned[k][d] for k, d in enumerate(offset)))
+        if offset[3] in turns:
+            action(*(turned[k][d] for k, d in enumerate(offset)))
 
 
 def device(z, y, core, x):
@@ -77,7 +81,7 @@
     def one(i):
         dst[rows8(i), :] = jnp.sum(blocks[i] * field, axis=0)
 
-    loop(N, one)
+    loop(N, one, N)
 
 
 def after(v):
@@ -116,41 +120,33 @@
     loop(tiles, one, 2)
 
 
-def spread_sum(lhs, wt, sums, count):
-    made = lax.dot_general(lhs[...], wt[...], (((1,), (1,)), ((), ())), preferred_element_type=F32)
+def spread_sum(lhs, wt, sums, base, count):
+    made = lax.dot_general(lhs, wt[...], (((1,), (1,)), ((), ())), preferred_element_type=F32)
     made = made[0:count] + made[count:]
-    sums[0, 0:count, :] = made[:, 0:128]
-    sums[1, 0:count, :] = made[:, 128:256]
-
-
-def messages(sums, count, row, out):
+    sums[0, base : base + count, :] = made[:, 0:128]
+    sums[1, base : base + count, :] = made[:, 128:256]
+
+
+def messages(sums, base, count, row, store):
     for half in range(2):
-        sums[half, pl.ds(N, count, stride=16), :] = jnp.broadcast_to(row, (count, 128))
+        sums[half, pl.ds(base + N, count, stride=16), :] = jnp.broadcast_to(row, (count, 128))
+    for hp in range(count // 2):
+        for half in range(2):
+            made = regroup([sums[half, pl.ds(base + hp * 32 + jj, 8, stride=4), :] for jj in range(4)])
+            for tl in range(4):
+                store(half * 4 + tl, hp, made[tl])
+
+
+def regroup(v):
     group = iota((8, 128), 1) // 32
-
-    def one(hp):
-        for half in range(2):
-            made = [None] * 4
-            for jj in range(4):
-                v = sums[half, pl.ds(hp * 32 + jj, 8, stride=4), :]
-                for tl in range(4):
-                    turn = ((jj - tl) % 4) * 32
-                    moved = pltpu.roll(v, turn, axis=1) if turn else v
-                    made[tl] = moved if jj == 0 else jnp.where(group == jj, moved, made[tl])
-            for tl in range(4):
-                out[half * 4 + tl, rows8(hp), :] = made[tl]
-
-    loop(count // 2, one, 2)
-
-
-def regroup(parts, jj):
-    group = iota((8, 128), 1) // 32
-    made = None
-    for tl in range(4):
-        turn = ((tl - jj) % 4) * 32
-        moved = pltpu.roll(parts[tl], turn, axis=1) if turn else parts[tl]
-        made = moved if tl == 0 else jnp.where(group == tl, moved, made)
-    return made
+    low, even = group < 2, group % 2 == 0
+    a = [jnp.where(low, v[i], pltpu.roll(v[i + 2], 64, axis=1)) for i in range(2)]
+    a += [jnp.where(low, pltpu.roll(v[i], 64, axis=1), v[i + 2]) for i in range(2)]
+    out = []
+    for i in (0, 2):
+        out.append(jnp.where(even, a[i], pltpu.roll(a[i + 1], 32, axis=1)))
+        out.append(jnp.where(even, pltpu.roll(a[i], 96, axis=1), a[i + 1]))
+    return out
 
 
 def scalar_of(v):
@@ -163,7 +159,7 @@
     out,
     slot_row, slot8, cid8, damp, pf_row, ps_row, pf16, ps16,
     mb, tb, blk, r3, z2, d2, mv, ez, e2, jv, near, far, f2, b2, tab, tab2, sums,
-    wt_s, oh_s, lhs_s, wt_p, oh_p, lhs_p, lam, out_f, out_b, recv_f, recv_b,
+    wt_s, oh_s, lhs_s, wt_p, oh_p, parts_p, lhs_p, lam, out_f, out_b, recv_f, recv_b,
     load_sem, send_sem, recv_sem,
 ):
     tm = lax.axis_index("tm")
@@ -213,24 +209,38 @@
     def halo(ph, who):
         return recv_f[ph, (who // 4) % 8, pl.ds(((who % 4) * 4 + who // 32) * 4 + 3, 1), :]
 
-    rz = None
-    for ph in range(2):
-        if ph == 0:
+    out[...] = jnp.zeros_like(out)
+    for field in (d2, e2, near, far):
+        field[...] = jnp.zeros_like(field)
+
+    def phase(ph, rz):
+        @pl.when(ph == 0)
+        def _():
             for copy in load_m:
                 copy.wait()
             load_blk.start()
+
         multiply(mb, r3, z2)
         z3 = z2[0:120, :].reshape(N, 8, 128)
         part = total(r3[0:N] * z3)
-        if ph == 0:
+
+        @pl.when(ph == 0)
+        def _():
             for copy in load_t:
                 copy.wait()
+
         multiply(tb, z3, mv)
         row = extras(z2, mv, part)
         fill(z2, 8, 8, 0, 4, oh_s, lhs_s)
-        spread_sum(lhs_s, wt_s, sums, 64)
-        messages(sums, 4, row, out_f.at[ph])
-        if ph == 0:
+        spread_sum(lhs_s[...], wt_s, sums, 0, 64)
+
+        def keep_f(tl, hp, v):
+            out_f[ph, tl, hp * 8 : (hp + 1) * 8, :] = v
+
+        messages(sums, 0, 4, row, keep_f)
+
+        @pl.when(ph == 0)
+        def _():
             pl.semaphore_wait(bar, 127)
 
         def send_f(z, y, core, x):
@@ -238,20 +248,21 @@
                 out_f.at[ph, y * 2 + core, rows4(z), :],
                 recv_f.at[ph, my_tl, rows4(my_x * 4 + my_z), :],
                 send_sem.at[ph, 0],
-                recv_sem.at[ph, 0],
+                recv_sem.at[ph, my_x],
                 device_id=device(z, y, core, x),
                 device_id_type=MESHID,
             ).start()
 
         sweep(send_f)
         pltpu.make_async_copy(
-            out_f.at[ph, my_tl, rows4(my_z), :], recv_f.at[ph, my_tl, rows4(my_x * 4 + my_z), :], recv_sem.at[ph, 0]
+            out_f.at[ph, my_tl, rows4(my_z), :], recv_f.at[ph, my_tl, rows4(my_x * 4 + my_z), :], recv_sem.at[ph, my_x]
         ).start()
 
         for j in range(N):
             at = slice(j * 8, (j + 1) * 8)
             ez[at, :] = jnp.where(pos_last, 0.0, after(z2[at, :])) - mv[at, :]
-        if ph == 0:
+        @pl.when(ph == 0)
+        def _():
             for copy in load_small[1:]:
                 copy.wait()
 
@@ -276,31 +287,28 @@
                     lam[h * 4 + tl, th * 4 : (th + 1) * 4, :] = jnp.where(spare, 0.0, jnp.broadcast_to(wide[t4 : t4 + 1, :], (4, 128)))
             load_blk.wait()
 
-        pltpu.make_async_copy(recv_f.at[ph], recv_f.at[ph], recv_sem.at[ph, 0]).wait()
+        for c in range(4):
+            block = recv_f.at[ph, :, c * 16 : (c + 1) * 16, :]
+            pltpu.make_async_copy(block, block, recv_sem.at[ph, c]).wait()
 
         def tables(hp):
             for h in range(2):
-                parts = [recv_f[ph, h * 4 + tl, rows8(hp), :] for tl in range(4)]
+                parts = regroup([recv_f[ph, h * 4 + tl, rows8(hp), :] for tl in range(4)])
                 for jj in range(4):
-                    tab[jj, h, rows8(hp), :] = regroup(parts, jj)
-
-        loop(8, tables, 2)
+                    tab[jj, h, rows8(hp), :] = parts[jj]
+
+        loop(8, tables, 8)
         rz_new = scalar_of(tab[3, 0]) + scalar_of(tab[3, 1])
-        nxt, prv = halo(ph, following), halo(ph, previous)
-        if ph == 0:
-            rz = rz_new
-            d2[...] = z2[...]
-        else:
-            beta = rz_new / rz
-            rz = rz_new
-            prv = prv + beta * halo(0, previous)
-            d2[...] = z2[...] + beta * d2[...]
+        beta = jnp.where(ph == 0, 0.0, rz_new / rz)
+        rz = rz_new
+        nxt = halo(ph, following)
+        prv = halo(ph, previous) + beta * halo(0, previous)
+        d2[...] = z2[...] + beta * d2[...]
         part = jnp.zeros((8, 128), F32)
         for j in range(N):
             at = slice(j * 8, (j + 1) * 8)
             v = (ez[at, :] + jnp.where(pos_last, spread(nxt, j + 96), 0.0)) * keep_last
-            if ph == 1:
-                v = v + beta * e2[at, :]
+            v = v + beta * e2[at, :]
             e2[at, :] = v
             part = part + v * v
         part = total(part)
@@ -327,8 +335,7 @@
             for j in range(N):
                 for pv in range(2):
                     v = found[j * 2 + pv]
-                    if ph == 1:
-                        v = v + beta * field[j, pv * 8 : (pv + 1) * 8, :]
+                    v = v + beta * field[j, pv * 8 : (pv + 1) * 8, :]
                     field[j, pv * 8 : (pv + 1) * 8, :] = v
 
         def forward(i):
@@ -340,33 +347,62 @@
             b2[rows16(j), :] = -jnp.sum(blk[:, j] * f2[0:240, :].reshape(N, 16, 128), axis=0)
 
         loop(N, backward, 3)
-        own = recv_f[ph, :, rows16(cl), :]
-        if ph == 1:
-            own = own + beta * recv_f[0, :, rows16(cl), :]
+        own = recv_f[ph, :, rows16(cl), :] + beta * recv_f[0, :, rows16(cl), :]
         damped = own * lam[...]
         part = part + total((f2[0:240, :] * f2[0:240, :]).reshape(N, 16, 128)) + total(damped * own)
-        fill(f2, 16, 16, 0, 16, oh_p, lhs_p)
-        fill(b2, 16, 16, 16, 16, oh_p, lhs_p)
-        spread_sum(lhs_p, wt_p, sums, 256)
         row = jnp.where(iota((1, 128), 1) % 32 == 30, part, 0.0)
-        messages(sums, 16, row, out_b.at[ph])
-        out_b[ph, :, rows16(cl), :] = out_b[ph, :, rows16(cl), :] + damped
-
-        def send_b(z, y, core, x):
-            pltpu.make_async_remote_copy(
-                out_b.at[ph, y * 2 + core, rows4(x * 4 + z), :],
-                recv_b.at[ph, lax.rem(my_tl, 4), my_x, rows4(my_z * 2 + lax.div(my_tl, 4)), :],
-                send_sem.at[ph, 1],
-                recv_sem.at[ph, 1],
-                device_id=device(z, y, core, x),
-                device_id_type=MESHID,
-            ).start()
-
-        sweep(send_b)
+        for base, src in ((0, f2), (16, b2)):
+            for a in range(16):
+                v = src[pl.ds(a, 16, stride=16), :]
+                high = v.astype(BF16)
+                cols = slice((base + a) * 128, (base + a + 1) * 128)
+                parts_p[0, :, cols] = high
+                parts_p[1, :, cols] = (v - high.astype(F32)).astype(BF16)
+
+        def fill_for(k, group):
+            for a in range(32):
+                cols = slice(a * 128, (a + 1) * 128)
+                both = [parts_p[n, :, cols] for n in range(2)]
+                for i, c in enumerate(group):
+                    for n in range(4):
+                        mask = oh_p[rows16(c * 4 + n), cols]
+                        for m in range(2):
+                            at = ((k * 2 + m) * len(group) + i) * 64 + n * 16
+                            lhs_p[at : at + 16, cols] = both[m] * mask
+
+        turns = TURNS
+        xs = [[lax.rem(my_x + turn, 4) for turn in group] for group in turns]
+        wide = len(turns[0]) * 64
+        fill_for(0, xs[0])
+        for k, group in enumerate(turns):
+            if k + 1 < len(turns):
+                fill_for(k + 1, xs[k + 1])
+            spread_sum(lhs_p[k * 2 * wide : (k + 1) * 2 * wide, :], wt_p, sums, k * wide, wide)
+
+            for i, turn in enumerate(group):
+
+                def keep_b(tl, hp, v):
+                    if turn == 0:
+                        v = v + damped[tl, hp * 8 : (hp + 1) * 8, :]
+                    out_b[ph, tl, rows8(xs[k][i] * 2 + hp), :] = v
+
+                messages(sums, k * wide + i * 64, 4, row, keep_b)
+
+            def send_b(z, y, core, x):
+                pltpu.make_async_remote_copy(
+                    out_b.at[ph, y * 2 + core, rows4(x * 4 + z), :],
+                    recv_b.at[ph, lax.rem(my_tl, 4), my_x, rows4(my_z * 2 + lax.div(my_tl, 4)), :],
+                    send_sem.at[ph, 1],
+                    recv_sem.at[ph, 4],
+                    device_id=device(z, y, core, x),
+                    device_id_type=MESHID,
+                ).start()
+
+            sweep(send_b, group)
         pltpu.make_async_copy(
             out_b.at[ph, my_tl, rows4(my_x * 4 + my_z), :],
             recv_b.at[ph, lax.rem(my_tl, 4), my_x, rows4(my_z * 2 + lax.div(my_tl, 4)), :],
-            recv_sem.at[ph, 1],
+            recv_sem.at[ph, 4],
         ).start()
 
         errors = e2[0:120, :].reshape(N, 8, 128)
@@ -378,12 +414,12 @@
 
         loop(N, inertial, 3)
 
-        pltpu.make_async_copy(recv_b.at[ph], recv_b.at[ph], recv_sem.at[ph, 1]).wait()
+        pltpu.make_async_copy(recv_b.at[ph], recv_b.at[ph], recv_sem.at[ph, 4]).wait()
 
         def tables2(gp):
-            parts = [jnp.sum(recv_b[ph, gl, :, rows8(gp), :], axis=0) for gl in range(4)]
+            parts = regroup([jnp.sum(recv_b[ph, gl, :, rows8(gp), :], axis=0) for gl in range(4)])
             for jj in range(4):
-                tab2[jj, rows8(gp), :] = regroup(parts, jj)
+                tab2[jj, rows8(gp), :] = parts[jj]
 
         loop(4, tables2, 4)
         alpha = rz / scalar_of(tab2[3])
@@ -396,9 +432,11 @@
                 found = jnp.where(high == g4, jnp.take_along_axis(src, low, axis=1), found)
             at = slice(j * 8, (j + 1) * 8)
             step = alpha * d2[at, :]
-            out[0, j] = step if ph == 0 else out[0, j] + step
+            out[0, j] = out[0, j] + step
             r3[j] = r3[j] - alpha * (v + found)
-
+        return rz
+
+    lax.fori_loop(0, 2, phase, jnp.ones((1, 1), F32))
     out[1] = r3[...]
     for ph in range(2):
         for way in range(2):
@@ -425,7 +463,7 @@
     whole = jnp.int32
     both = pl.pallas_call(
         kernel,
-        out_shape=jax.ShapeDtypeStruct((2, 16, 8, 128), F32),
+        out_shape=pltpu.VMEM((2, 16, 8, 128), F32),
         in_specs=[anywhere] * 12,
         out_specs=vm,
         scratch_shapes=[
@@ -448,6 +486,7 @@
             pltpu.VMEM((128, 1024), BF16),
             pltpu.VMEM((256, 4096), BF16),
             pltpu.VMEM((256, 4096), BF16),
+            pltpu.VMEM((2, 16, 4096), BF16),
             pltpu.VMEM((512, 4096), BF16),
             pltpu.VMEM((8, 16, 128), F32),
             pltpu.VMEM((2, 8, 16, 128), F32),
@@ -456,7 +495,7 @@
             pltpu.VMEM((2, 4, 4, 32, 128), F32),
             pltpu.SemaphoreType.DMA((5, 8)),
             pltpu.SemaphoreType.DMA((2, 2)),
-            pltpu.SemaphoreType.DMA((2, 2)),
+            pltpu.SemaphoreType.DMA((2, 5)),
         ],
         compiler_params=pltpu.CompilerParams(collective_id=0, has_side_effects=True, vmem_limit_bytes=60 * 1024 * 1024),
     )(
@@ -479,7 +518,7 @@
         in_specs=[vm],
         out_specs=(anywhere, anywhere),
         scratch_shapes=[pltpu.SemaphoreType.DMA((2, 8))],
-    )(both)
+    )(pltpu.with_memory_space_constraint(both, pltpu.VMEM))
 
 
 def solution(mesh):

time: 59.7 us -> 52.8 us (0.88)
  Pallas kernels: 58.9 us -> 52 us
    pallas_call x1, Pallas kernels: 57.1 us -> 51.1 us  [on_device(): pl.pallas_call(kernel, out_shape=pltpu.VMEM((2, 16, 8, 128), F32), in_spe...]
    pallas_call x1, Pallas kernels: 1.75 us -> 0.85 us  [on_device(): pl.pallas_call(finish, out_shape=(jax.ShapeDtypeStruct((N, 1024), F32),)...]
where the time goes in v3:
time: 52.8 us; the launch traced here: 52.6 us
  Pallas kernels  52 us (98%)
  between operations  0.64 us (1%)
    pallas_call x1, Pallas kernels, on_device(): pl.pallas_call(kernel, out_shape=pltpu.VMEM((2, 16, 8, 128), F32), in_spe...  51.1 us

profile of v3, /device:TPU:1, one launch (start us, length us, event | category | flops | bytes accessed | tf_op | source)
XLA Modules:
  0.0 52.6 jit_solution(5875742400634660581)
XLA Ops:
  0.6 51.1 %shard_map.104.both = f32[2,16,8,128]{3,2,1,0:T(8,128)S(1)} custom-call(f32[15,1024]{1,0:T(8,128)} %b_any.1, s32[1,1024]{1,0:T(1,128)} %bitcast.9, s32[8,128]{1,0:T(8,128)} %bitcast.10, s32[8,128]{1,0:T(8,128)} %bitcast.11, f32[1,64]{1,0:T(1,128)} %damp_any.1, s32[1,2048]{1,0:T(1,128)} %pf_any.1, s32[1,2048]{1,0:T(1,128)} %ps_any.1, s32[16,128]{1,0:T(8,128)} %bitcast.7, ...), custom_call_target="tpu_custom_call" | custom-call | tf_op jit(solution)/shard_map/pallas_call | solution.py:464
  51.8 0.8 %shard_map.105 = (f32[15,1024]{1,0:T(8,128)}, f32[15,1024]{1,0:T(8,128)}) custom-call(f32[2,16,8,128]{3,2,1,0:T(8,128)S(1)} %shard_map.104.both), custom_call_target="tpu_custom_call" | custom-call | tf_op jit(solution)/shard_map/pallas_call | solution.py:515

commit v4 on v3

--- a/solution.py
+++ b/solution.py
@@ -19,9 +19,6 @@
     ((z, y, c, x) for z in range(4) for y in range(4) for c in range(2) for x in range(4) if z or y or c or x),
     key=lambda o: -hops(o[0]) - hops(o[1]) - hops(o[3]),
 )
-
-
-TURNS = ((2, 1, 3, 0),)
 
 
 def place():
@@ -159,7 +156,7 @@
     out,
     slot_row, slot8, cid8, damp, pf_row, ps_row, pf16, ps16,
     mb, tb, blk, r3, z2, d2, mv, ez, e2, jv, near, far, f2, b2, tab, tab2, sums,
-    wt_s, oh_s, lhs_s, wt_p, oh_p, parts_p, lhs_p, lam, out_f, out_b, recv_f, recv_b,
+    wt_s, oh_s, lhs_s, wt_p, oh_p, lhs_p, lam, out_f, out_b, recv_f, recv_b,
     load_sem, send_sem, recv_sem,
 ):
     tm = lax.axis_index("tm")
@@ -331,7 +328,7 @@
                                 carry[k] = jnp.where(here[pv], jnp.take_along_axis(src, low[pv], axis=1), carry[k])
                 return tuple(carry)
 
-            found = lax.fori_loop(0, 4, look, tuple(jnp.zeros((8, 128), F32) for _ in range(30)))
+            found = lax.fori_loop(0, 4, look, tuple(jnp.zeros((8, 128), F32) for _ in range(30)), unroll=2)
             for j in range(N):
                 for pv in range(2):
                     v = found[j * 2 + pv]
@@ -341,64 +338,44 @@
         def forward(i):
             f2[rows16(i), :] = near[i] - jnp.sum(blk[i] * far[...], axis=0)
 
-        loop(N, forward, 3)
+        loop(N, forward, N)
 
         def backward(j):
             b2[rows16(j), :] = -jnp.sum(blk[:, j] * f2[0:240, :].reshape(N, 16, 128), axis=0)
 
-        loop(N, backward, 3)
+        loop(N, backward, N)
         own = recv_f[ph, :, rows16(cl), :] + beta * recv_f[0, :, rows16(cl), :]
         damped = own * lam[...]
         part = part + total((f2[0:240, :] * f2[0:240, :]).reshape(N, 16, 128)) + total(damped * own)
         row = jnp.where(iota((1, 128), 1) % 32 == 30, part, 0.0)
-        for base, src in ((0, f2), (16, b2)):
-            for a in range(16):
-                v = src[pl.ds(a, 16, stride=16), :]
-                high = v.astype(BF16)
-                cols = slice((base + a) * 128, (base + a + 1) * 128)
-                parts_p[0, :, cols] = high
-                parts_p[1, :, cols] = (v - high.astype(F32)).astype(BF16)
-
-        def fill_for(k, group):
-            for a in range(32):
-                cols = slice(a * 128, (a + 1) * 128)
-                both = [parts_p[n, :, cols] for n in range(2)]
-                for i, c in enumerate(group):
-                    for n in range(4):
-                        mask = oh_p[rows16(c * 4 + n), cols]
-                        for m in range(2):
-                            at = ((k * 2 + m) * len(group) + i) * 64 + n * 16
-                            lhs_p[at : at + 16, cols] = both[m] * mask
-
-        turns = TURNS
-        xs = [[lax.rem(my_x + turn, 4) for turn in group] for group in turns]
-        wide = len(turns[0]) * 64
-        fill_for(0, xs[0])
-        for k, group in enumerate(turns):
-            if k + 1 < len(turns):
-                fill_for(k + 1, xs[k + 1])
-            spread_sum(lhs_p[k * 2 * wide : (k + 1) * 2 * wide, :], wt_p, sums, k * wide, wide)
-
-            for i, turn in enumerate(group):
-
-                def keep_b(tl, hp, v):
-                    if turn == 0:
-                        v = v + damped[tl, hp * 8 : (hp + 1) * 8, :]
-                    out_b[ph, tl, rows8(xs[k][i] * 2 + hp), :] = v
-
-                messages(sums, k * wide + i * 64, 4, row, keep_b)
-
-            def send_b(z, y, core, x):
-                pltpu.make_async_remote_copy(
-                    out_b.at[ph, y * 2 + core, rows4(x * 4 + z), :],
-                    recv_b.at[ph, lax.rem(my_tl, 4), my_x, rows4(my_z * 2 + lax.div(my_tl, 4)), :],
-                    send_sem.at[ph, 1],
-                    recv_sem.at[ph, 4],
-                    device_id=device(z, y, core, x),
-                    device_id_type=MESHID,
-                ).start()
-
-            sweep(send_b, group)
+        for a in range(32):
+            cols = slice(a * 128, (a + 1) * 128)
+            v = (f2, b2)[a // 16][pl.ds(a % 16, 16, stride=16), :]
+            high = v.astype(BF16)
+            both = (high, (v - high.astype(F32)).astype(BF16))
+            for n in range(16):
+                mask = oh_p[n * 16 : (n + 1) * 16, cols]
+                for m in range(2):
+                    lhs_p[m * 256 + n * 16 : m * 256 + (n + 1) * 16, cols] = both[m] * mask
+        spread_sum(lhs_p[...], wt_p, sums, 0, 256)
+
+        def keep_b(tl, hp, v):
+            out_b[ph, tl, hp * 8 : (hp + 1) * 8, :] = v
+
+        messages(sums, 0, 16, row, keep_b)
+        out_b[ph, :, rows16(my_x), :] = out_b[ph, :, rows16(my_x), :] + damped
+
+        def send_b(z, y, core, x):
+            pltpu.make_async_remote_copy(
+                out_b.at[ph, y * 2 + core, rows4(x * 4 + z), :],
+                recv_b.at[ph, lax.rem(my_tl, 4), my_x, rows4(my_z * 2 + lax.div(my_tl, 4)), :],
+                send_sem.at[ph, 1],
+                recv_sem.at[ph, 4],
+                device_id=device(z, y, core, x),
+                device_id_type=MESHID,
+            ).start()
+
+        sweep(send_b)
         pltpu.make_async_copy(
             out_b.at[ph, my_tl, rows4(my_x * 4 + my_z), :],
             recv_b.at[ph, lax.rem(my_tl, 4), my_x, rows4(my_z * 2 + lax.div(my_tl, 4)), :],
@@ -486,7 +463,6 @@
             pltpu.VMEM((128, 1024), BF16),
             pltpu.VMEM((256, 4096), BF16),
             pltpu.VMEM((256, 4096), BF16),
-            pltpu.VMEM((2, 16, 4096), BF16),
             pltpu.VMEM((512, 4096), BF16),
             pltpu.VMEM((8, 16, 128), F32),
             pltpu.VMEM((2, 8, 16, 128), F32),

time: 52.8 us -> 51.7 us (0.979)
  Pallas kernels: 52 us -> 50.9 us
    pallas_call x1, Pallas kernels: 51.1 us -> 50.1 us  [on_device(): pl.pallas_call(kernel, out_shape=pltpu.VMEM((2, 16, 8, 128), F32), in_spe...]
where the time goes in v4:
time: 51.7 us; the launch traced here: 51.5 us
  Pallas kernels  50.9 us (98%)
  between operations  0.64 us (1%)
    pallas_call x1, Pallas kernels, on_device(): pl.pallas_call(kernel, out_shape=pltpu.VMEM((2, 16, 8, 128), F32), in_spe...  50.1 us

profile of v4, /device:TPU:1, one launch (start us, length us, event | category | flops | bytes accessed | tf_op | source)
XLA Modules:
  0.0 51.5 jit_solution(4296384834768285442)
XLA Ops:
  0.6 50.1 %shard_map.104.both = f32[2,16,8,128]{3,2,1,0:T(8,128)S(1)} custom-call(f32[15,1024]{1,0:T(8,128)} %b_any.1, s32[1,1024]{1,0:T(1,128)} %bitcast.9, s32[8,128]{1,0:T(8,128)} %bitcast.10, s32[8,128]{1,0:T(8,128)} %bitcast.11, f32[1,64]{1,0:T(1,128)} %damp_any.1, s32[1,2048]{1,0:T(1,128)} %pf_any.1, s32[1,2048]{1,0:T(1,128)} %ps_any.1, s32[16,128]{1,0:T(8,128)} %bitcast.7, ...), custom_call_target="tpu_custom_call" | custom-call | tf_op jit(solution)/shard_map/pallas_call | solution.py:441
  50.7 0.8 %shard_map.105 = (f32[15,1024]{1,0:T(8,128)}, f32[15,1024]{1,0:T(8,128)}) custom-call(f32[2,16,8,128]{3,2,1,0:T(8,128)S(1)} %shard_map.104.both), custom_call_target="tpu_custom_call" | custom-call | tf_op jit(solution)/shard_map/pallas_call | solution.py:491
